TPU v7x, 512 devices: a whole 4x4x16 slice. The times are simulated.
512 devices in a mesh: dp: 8 (over y, x_lo), expert: 64 (over z, x_hi, core).
Axes of the slice: x: 4 (x_hi: 2, x_lo: 2; x = x_hi * 2 + x_lo), y: 4, z: 16, core: 2. Of those that a mesh axis runs over, the one named last changes fastest.
Arguments:
- tokens: bfloat16 [65536, 2048], P(('dp', 'expert')), may hold values from -6 to 6
- routes: int32 [65536, 2], P(('dp', 'expert')), may hold values from 0 to 63, all different within a row; in each aligned block of 128 rows (0 to 127, 128 to 255, ...) at most 6 rows name the same one
- gates: float32 [65536, 2], P(('dp', 'expert')), may hold values from 0.05 to 1
- grad_out: bfloat16 [65536, 2048], P(('dp', 'expert')), may hold values from -6 to 6
- w_gate: bfloat16 [64, 2048, 768], P('expert', 'dp'), may hold values from -0.125 to 0.125
- w_up: bfloat16 [64, 2048, 768], P('expert', 'dp'), may hold values from -0.125 to 0.125
- w_down: bfloat16 [64, 768, 2048], P('expert', None, 'dp'), may hold values from -0.21875 to 0.21875
Outputs:
- grad_tokens: bfloat16 [65536, 2048], P(('dp', 'expert'))
- grad_gates: float32 [65536, 2], P(('dp', 'expert'))
- grad_down: float32 [64, 768, 2048], P('expert', None, 'dp')
Inputs may be any that keep to these rules, and one draw needn't show every extreme that they name: Within the rows of one device no expert is named by more than 6 routes, a bound that some block reaches; the 2 experts of a token differ.
All inputs are finite; a program needn't handle non-finite values.
Results may differ from a plain program's by a relative error of at most 0.015.
Values may be sent and summed in bfloat16 or wider, within the bound.
A program may use at most 128 MiB of HBM per device.

v0:
```python
import jax
import jax.numpy as jnp
from jax import lax
from jax.sharding import PartitionSpec as P


def silu_parts(pre):
    sig = jax.nn.sigmoid(pre)
    return (pre * sig, sig * (1.0 + pre * (1.0 - sig)))


def contract_last(left, right):
    return lax.dot_general(
        left, right, (((1,), (1,)), ((), ())), preferred_element_type=jnp.float32
    )


def contract_first(left, right):
    return lax.dot_general(
        left, right, (((0,), (0,)), ((), ())), preferred_element_type=jnp.float32
    )


def full_weights(w_gate, w_up, w_down):
    gathered = (
        lax.all_gather(w_gate, "dp", axis=1, tiled=True),
        lax.all_gather(w_up, "dp", axis=1, tiled=True),
    )
    down_full = lax.all_gather(w_down, "dp", axis=2, tiled=True)[0]
    return (gathered[0][0], gathered[1][0], down_full)


def expert_rows(x_rows, scaled, gate_full, up_full, down_full):
    pre_gate = jnp.dot(x_rows, gate_full, preferred_element_type=jnp.float32)
    pre_up = jnp.dot(x_rows, up_full, preferred_element_type=jnp.float32)
    act, slope = silu_parts(pre_gate)
    hidden_f = act * pre_up
    back = contract_last(scaled, down_full)
    score = jnp.sum(back * hidden_f, axis=1).astype(jnp.bfloat16)
    d_gate = (back * pre_up * slope).astype(jnp.bfloat16)
    d_up = (back * act).astype(jnp.bfloat16)
    route_grad = (contract_last(d_gate, gate_full) + contract_last(d_up, up_full)).astype(
        jnp.bfloat16
    )
    return (route_grad, score, hidden_f.astype(jnp.bfloat16))


def per_device(tokens, routes, gates, grad_out, w_gate, w_up, w_down):
    experts = lax.axis_size("expert")
    count = tokens.shape[0]
    width = tokens.shape[1]
    top = routes.shape[1]
    cap = 3 * count * top // (2 * experts)
    slots = experts * cap
    routed = count * top
    flat = routes.reshape(routed)
    labels = jnp.arange(experts, dtype=jnp.int32)
    onehot = (flat[:, None] == labels[None, :]).astype(jnp.int32)
    rank = jnp.sum((jnp.cumsum(onehot, axis=0) - onehot) * onehot, axis=1)
    position = flat * cap + rank
    owner = (
        jnp.full((slots,), routed, jnp.int32).at[position].set(jnp.arange(routed, dtype=jnp.int32))
    )
    source = owner // top
    padded_tokens = jnp.concatenate([tokens, jnp.zeros((1, width), tokens.dtype)], axis=0)
    padded_grads = jnp.concatenate([grad_out, jnp.zeros((1, width), grad_out.dtype)], axis=0)
    padded_gates = jnp.concatenate([gates.reshape(routed), jnp.zeros((1,), jnp.float32)], axis=0)
    inputs_out = padded_tokens[source].reshape(experts, cap, width)
    scaled_out = (padded_gates[owner][:, None] * padded_grads[source].astype(jnp.float32)).astype(
        jnp.bfloat16
    )
    scaled_out = scaled_out.reshape(experts, cap, width)
    arrived = (
        lax.all_to_all(inputs_out, "expert", split_axis=0, concat_axis=0, tiled=True),
        lax.all_to_all(scaled_out, "expert", split_axis=0, concat_axis=0, tiled=True),
    )
    x_rows = arrived[0].reshape(slots, width)
    scaled_rows = arrived[1].reshape(slots, width)
    gate_full, up_full, down_full = full_weights(w_gate, w_up, w_down)
    route_grad, score, hidden = expert_rows(x_rows, scaled_rows, gate_full, up_full, down_full)
    down_share = lax.psum_scatter(
        contract_first(scaled_rows, hidden).astype(jnp.bfloat16),
        "dp",
        scatter_dimension=0,
        tiled=True,
    ).astype(jnp.float32)
    grad_down = jnp.transpose(down_share)[None]
    returned = (
        lax.all_to_all(
            route_grad.reshape(experts, cap, width),
            "expert",
            split_axis=0,
            concat_axis=0,
            tiled=True,
        ),
        lax.all_to_all(
            score.reshape(experts, cap), "expert", split_axis=0, concat_axis=0, tiled=True
        ),
    )
    back_rows = returned[0].reshape(slots, width)
    back_scores = returned[1].reshape(slots)
    per_route = back_rows[position].reshape(count, top, width)
    grad_tokens = jnp.sum(per_route.astype(jnp.float32), axis=1).astype(jnp.bfloat16)
    grad_gates = back_scores[position].astype(jnp.float32).reshape(count, top) / gates
    return (grad_tokens, grad_gates, grad_down)


def solution(mesh):
    placed = (
        P(("dp", "expert"), None),
        P(("dp", "expert"), None),
        P(("dp", "expert"), None),
        P(("dp", "expert"), None),
        P("expert", "dp", None),
        P("expert", "dp", None),
        P("expert", None, "dp"),
    )
    return jax.shard_map(
        per_device,
        mesh=mesh,
        in_specs=placed,
        out_specs=(P(("dp", "expert"), None), P(("dp", "expert"), None), P("expert", None, "dp")),
        check_vma=False,
    )
```

profile of v0, /device:TPU:1, one launch (start us, length us, event | category | flops | bytes accessed | tf_op | source)
XLA Modules:
  0.0 450.0 jit_solution(17397931720539439064)
XLA Ops:
  7.2 0.0 all-gather.8.cloned.1.call-start
  7.2 0.7 all-gather.8.cloned.1.call-update
  7.9 0.8 copy.21
  8.7 0.1 eq.29
  8.8 0.1 eq.25
  9.0 0.6 reduce-window.6
  9.6 0.2 slice_reduce_fusion
  9.8 0.7 broadcast_multiply_fusion
  10.5 0.1 copy.20
  10.6 0.1 mul.56
  10.8 1.1 concatenate.10
  11.9 0.1 fusion.18
  12.0 1.4 scatter_custom_fusion
  13.4 2.5 gather_fusion.1
  15.9 0.0 copy-start.2
  15.9 2.2 reshape.115
  18.1 0.0 copy-done.2
  18.1 0.1 copy.19
  18.2 0.1 reshape.106
  18.4 2.8 gather_fusion
  21.2 0.1 mul.58
  21.3 3.9 multiply_convert_fusion
  25.2 19.7 %all-to-all-start = ((bf16[64,6,2048]{2,1,0:T(8,128)(2,1)}), bf16[64,6,2048]{2,1,0:T(8,128)(2,1)S(1)}, u32[]{:S(2)}, u32[]{:S(2)}) async-start(bf16[64,6,2048]{2,1,0:T(8,128)(2,1)} %multiply_convert_fusion), calls=%async_computation | async-start | bytes 4194304 | tf_op jit(solution)/shard_map/all_to_all | solution.py:75
  44.9 0.0 all-gather.6.cloned.1.call-start
  45.0 0.7 all-gather.6.cloned.1.call-update
  45.7 3.1 gather_fusion.2
  48.8 3.7 reshape.109
  52.5 90.7 %all-to-all-done = bf16[64,6,2048]{2,1,0:T(8,128)(2,1)S(1)} async-done(((bf16[64,6,2048]{2,1,0:T(8,128)(2,1)}), bf16[64,6,2048]{2,1,0:T(8,128)(2,1)S(1)}, u32[]{:S(2)}, u32[]{:S(2)}) %all-to-all-start) | async-done | bytes 1572896 | tf_op jit(solution)/shard_map/all_to_all | solution.py:75
  143.3 8.2 %all-to-all-start.1 = ((bf16[64,6,2048]{2,1,0:T(8,128)(2,1)}), bf16[64,6,2048]{2,1,0:T(8,128)(2,1)}, u32[]{:S(2)}, u32[]{:S(2)}) async-start(bf16[64,6,2048]{2,1,0:T(8,128)(2,1)} %reshape.109), calls=%async_computation.1 | async-start | bytes 4194304 | tf_op jit(solution)/shard_map/all_to_all | solution.py:74
  151.5 0.2 all-gather.4.cloned.1.call-start
  151.7 0.5 all-gather.4.cloned.1.call-update
  152.2 1.4 reshape.108
  153.6 96.5 %all-to-all-done.1 = bf16[64,6,2048]{2,1,0:T(8,128)(2,1)} async-done(((bf16[64,6,2048]{2,1,0:T(8,128)(2,1)}), bf16[64,6,2048]{2,1,0:T(8,128)(2,1)}, u32[]{:S(2)}, u32[]{:S(2)}) %all-to-all-start.1) | async-done | bytes 1572896 | tf_op jit(solution)/shard_map/all_to_all | solution.py:74
  250.1 2.6 reshape.110
  252.8 0.0 all-gather.8.cloned.1.call-done
  252.8 4.3 fusion.2
  257.1 3.4 fusion.6
  260.6 1.1 copy-done.8
  261.6 0.0 copy-done
  261.7 3.7 convolution_convert_fusion
  265.3 26.6 %all-gather.4.cloned.1.call-done = bf16[1,768,2048]{2,1,0:T(8,128)(2,1)} async-done(((bf16[1,768,256]{2,1,0:T(8,128)(2,1)}), bf16[1,768,2048]{2,1,0:T(8,128)(2,1)}) %all-gather.4.cloned.1.call-update) | async-done | bytes 3145744 | tf_op jit(solution)/shard_map/all_gather | solution.py:29
  291.9 4.7 %multiply_reduce_fusion = (bf16[384]{0:T(512)(128)(2,1)S(1)}, f32[384,768]{1,0:T(8,128)}) fusion(f32[384,768]{1,0:T(8,128)} %copy-done.8, f32[384,768]{1,0:T(8,128)S(1)} %copy-done.5, bf16[384,2048]{1,0:T(8,128)(2,1)S(1)} %copy-done, bf16[1,768,2048]{2,1,0:T(8,128)(2,1)} %all-gather.4.cloned.1.call-done), kind=kOutput, calls=%fused_computation.19 | convolution fusion | flops 1210023552 | bytes 8258304 | tf_op jit(solution)/shard_map/dot_general | solution.py:13
  296.6 0.8 convert_element_type.73
  297.4 13.6 %all-to-all-start.3 = ((bf16[64,1,6]{2,1,0:T(2,128)(2,1)}), bf16[64,1,6]{2,1,0:T(2,128)(2,1)S(1)}, u32[]{:S(2)}, u32[]{:S(2)}) async-start(bf16[64,1,6]{2,1,0:T(2,128)(2,1)} %convert_element_type.73), calls=%async_computation.3 | async-start | bytes 65536 | tf_op jit(solution)/shard_map/all_to_all | solution.py:96
  311.1 0.0 reduce-scatter.2.cloned.1.call-start
  311.1 0.5 reduce-scatter.2.cloned.1.call-update
  311.6 0.7 copy-done.6
  312.3 3.9 fusion
  316.3 1.5 add_convert_fusion
  317.8 1.6 reshape.111
  319.4 6.3 %all-to-all-done.3 = bf16[64,1,6]{2,1,0:T(2,128)(2,1)S(1)} async-done(((bf16[64,1,6]{2,1,0:T(2,128)(2,1)}), bf16[64,1,6]{2,1,0:T(2,128)(2,1)S(1)}, u32[]{:S(2)}, u32[]{:S(2)}) %all-to-all-start.3) | async-done | bytes 800 | tf_op jit(solution)/shard_map/all_to_all | solution.py:96
  325.7 9.0 %all-to-all-start.2 = ((bf16[64,6,2048]{2,1,0:T(8,128)(2,1)}), bf16[64,6,2048]{2,1,0:T(8,128)(2,1)}, u32[]{:S(2)}, u32[]{:S(2)}) async-start(bf16[64,6,2048]{2,1,0:T(8,128)(2,1)} %reshape.111), calls=%async_computation.2 | async-start | bytes 4194304 | tf_op jit(solution)/shard_map/all_to_all | solution.py:89
  334.7 0.1 reduce.2
  334.8 0.1 reshape.114
  334.9 1.9 gather_fusion.4
  336.9 0.1 reshape.116
  337.0 0.6 copy.26
  337.7 95.3 %all-to-all-done.2 = bf16[64,6,2048]{2,1,0:T(8,128)(2,1)} async-done(((bf16[64,6,2048]{2,1,0:T(8,128)(2,1)}), bf16[64,6,2048]{2,1,0:T(8,128)(2,1)}, u32[]{:S(2)}, u32[]{:S(2)}) %all-to-all-start.2) | async-done | bytes 1572896 | tf_op jit(solution)/shard_map/all_to_all | solution.py:89
  433.0 2.6 reshape.112
  435.6 1.4 gather_fusion.3
  436.9 0.7 reshape.113
  437.7 3.6 reduce_sum.34
  441.3 1.0 convert_bitcast_fusion
  442.4 1.1 copy.27
  (26 shorter events, 0.2 us)
Async XLA Ops:
  7.2 245.6 %all-gather.8.cloned.1.call-start = ((), (), s32[]{:S(2)}) async-start(), calls=%async_computation.7 | async-start | bytes 3538944 | tf_op jit(solution)/shard_map/all_gather | solution.py:26
  15.9 2.2 copy-start.2
  25.2 20.5 %copy-start.1 = (bf16[128,2048]{1,0:T(8,128)(2,1)S(1)}, bf16[128,2048]{1,0:T(8,128)(2,1)}, u32[]{:S(2)}) copy-start(bf16[128,2048]{1,0:T(8,128)(2,1)} %param.7) | copy-start | bytes 1572868
  25.2 118.1 %all-to-all-start = ((bf16[64,6,2048]{2,1,0:T(8,128)(2,1)}), bf16[64,6,2048]{2,1,0:T(8,128)(2,1)S(1)}, u32[]{:S(2)}, u32[]{:S(2)}) async-start(bf16[64,6,2048]{2,1,0:T(8,128)(2,1)} %multiply_convert_fusion), calls=%async_computation | async-start | bytes 4194304 | tf_op jit(solution)/shard_map/all_to_all | solution.py:75
  44.9 212.2 %all-gather.6.cloned.1.call-start = ((), (), s32[]{:S(2)}) async-start(), calls=%async_computation.6 | async-start | bytes 3538944 | tf_op jit(solution)/shard_map/all_gather | solution.py:27
  143.3 106.9 %all-to-all-start.1 = ((bf16[64,6,2048]{2,1,0:T(8,128)(2,1)}), bf16[64,6,2048]{2,1,0:T(8,128)(2,1)}, u32[]{:S(2)}, u32[]{:S(2)}) async-start(bf16[64,6,2048]{2,1,0:T(8,128)(2,1)} %reshape.109), calls=%async_computation.1 | async-start | bytes 4194304 | tf_op jit(solution)/shard_map/all_to_all | solution.py:74
  151.5 140.4 %all-gather.4.cloned.1.call-start = ((), (), s32[]{:S(2)}) async-start(), calls=%async_computation.5 | async-start | bytes 3538944 | tf_op jit(solution)/shard_map/all_gather | solution.py:29
  257.1 4.6 %copy-start = (bf16[384,2048]{1,0:T(8,128)(2,1)S(1)}, bf16[384,2048]{1,0:T(8,128)(2,1)}, u32[]{:S(2)}) copy-start(bf16[384,2048]{1,0:T(8,128)(2,1)} %reshape.108) | copy-start | bytes 4718596
  257.1 4.6 %copy-start.4 = (f32[384,768]{1,0:T(8,128)S(1)}, f32[384,768]{1,0:T(8,128)}, u32[]{:S(2)}) copy-start(f32[384,768]{1,0:T(8,128)} %fusion.2) | copy-start | bytes 3538948
  260.5 1.1 copy-start.8
  261.7 30.2 %copy-start.5 = (f32[384,768]{1,0:T(8,128)S(1)}, f32[384,768]{1,0:T(8,128)}, u32[]{:S(2)}) copy-start(f32[384,768]{1,0:T(8,128)} %fusion.2) | copy-start | bytes 3538948
  297.4 28.3 %all-to-all-start.3 = ((bf16[64,1,6]{2,1,0:T(2,128)(2,1)}), bf16[64,1,6]{2,1,0:T(2,128)(2,1)S(1)}, u32[]{:S(2)}, u32[]{:S(2)}) async-start(bf16[64,1,6]{2,1,0:T(2,128)(2,1)} %convert_element_type.73), calls=%async_computation.3 | async-start | bytes 65536 | tf_op jit(solution)/shard_map/all_to_all | solution.py:96
  311.1 1.3 copy-start.6
  311.1 130.2 %reduce-scatter.2.cloned.1.call-start = ((), (), s32[]{:S(2)}) async-start(), calls=%async_computation.8 | async-start | bytes 3538944 | tf_op jit(solution)/shard_map/reduce_scatter | solution.py:81
  312.3 3.9 copy-start.3
  312.3 3.9 copy-start.7
  325.7 107.3 %all-to-all-start.2 = ((bf16[64,6,2048]{2,1,0:T(8,128)(2,1)}), bf16[64,6,2048]{2,1,0:T(8,128)(2,1)}, u32[]{:S(2)}, u32[]{:S(2)}) async-start(bf16[64,6,2048]{2,1,0:T(8,128)(2,1)} %reshape.111), calls=%async_computation.2 | async-start | bytes 4194304 | tf_op jit(solution)/shard_map/all_to_all | solution.py:89
Sparse Core Ops, SparseCore 0:
  10.1 99.9 all-gather.7
  112.1 93.5 all-gather.5
  207.8 84.0 all-gather.3
  314.4 96.6 reduce-scatter.1
where the time goes:
time: 453 us; the launch traced here: 450 us
  waiting for transfers between devices  318 us (70%)
  starting transfers between devices  50.9 us (11%)
  local copies, waits for them, and re-layouts  35.6 us (8%)
  matrix products  21.5 us (5%)
  between operations  14.1 us (3%)
  other arithmetic  10.1 us (2%)
    all_to_all x1, waiting for transfers between devices, per_device(): lax.all_to_all(inputs_out, 'expert', split_axis=0, concat_axis=0, tiled=T...  96.5 us
    all_to_all x1, waiting for transfers between devices, per_device(): lax.all_to_all(route_grad.reshape(experts, cap, width), 'expert', split_a...  95.3 us
    all_to_all x1, waiting for transfers between devices, per_device(): lax.all_to_all(scaled_out, 'expert', split_axis=0, concat_axis=0, tiled=T...  90.7 us
    all_gather x1, waiting for transfers between devices, full_weights(): down_full = lax.all_gather(w_down, 'dp', axis=2, tiled=True)[0]  26.6 us
    all_to_all x1, starting transfers between devices, per_device(): lax.all_to_all(scaled_out, 'expert', split_axis=0, concat_axis=0, tiled=T...  19.7 us
    all_to_all x1, starting transfers between devices, per_device(): lax.all_to_all(score.reshape(experts, cap), 'expert', split_axis=0, conca...  13.6 us
    dot_general x3, matrix products, contract_last(): lax.dot_general(left, right, (((1,), (1,)), ((), ())), preferred_element_...  10.1 us
  transfers between devices with their start and end apart: 8, of which 5 were waited for; matrix products, arithmetic and copies ran while one was open for 13% of the time, Pallas kernels for 0%

commit v1 on v0

v1 whole, which is shorter than its diff:
```python
import functools

import jax
import jax.numpy as jnp
from jax import lax
from jax.experimental import pallas as pl
from jax.experimental.pallas import tpu as pltpu
from jax.sharding import PartitionSpec as P


def silu_parts(pre):
    sig = jax.nn.sigmoid(pre)
    return (pre * sig, sig * (1.0 + pre * (1.0 - sig)))


def contract_last(left, right):
    return lax.dot_general(
        left, right, (((1,), (1,)), ((), ())), preferred_element_type=jnp.float32
    )


def xfer_kernel(plan, sizes, *refs):
    count = len(plan)
    srcs, dsts = refs[:count], refs[count:2 * count]
    send, recv, own = refs[2 * count:2 * count + 3]
    me_dp = lax.axis_index("dp")
    me_ex = lax.axis_index("expert")
    mine = {"dp": me_dp, "expert": me_ex}

    def block(i, peer):
        return srcs[i].at[peer] if plan[i][0] == "a2a" else srcs[i]

    def remote(i, peer, slot):
        axis = plan[i][1]
        device = (peer, me_ex) if axis == "dp" else (me_dp, peer)
        return pltpu.make_async_remote_copy(
            src_ref=block(i, peer),
            dst_ref=dsts[i].at[slot],
            send_sem=send.at[i, peer],
            recv_sem=recv.at[i, slot],
            device_id=device,
            device_id_type=pl.DeviceIdType.MESH,
        )

    local = []
    for i, (kind, axis) in enumerate(plan):
        me = mine[axis]
        copy = pltpu.make_async_copy(block(i, me), dsts[i].at[me], own.at[i])
        copy.start()
        local.append(copy)
    for i, (kind, axis) in enumerate(plan):
        me, n = mine[axis], sizes[axis]

        @pl.loop(1, n)
        def _(j):
            peer = lax.rem(me + j, n)
            remote(i, peer, me).start()

    for i, (kind, axis) in enumerate(plan):
        me, n = mine[axis], sizes[axis]

        @pl.loop(1, n)
        def _(j):
            peer = lax.rem(me + j, n)
            remote(i, peer, me).wait_send()
            remote(i, peer, peer).wait_recv()

    for copy in local:
        copy.wait()


def exchange(plan, sizes, srcs, dst_shapes):
    count = len(plan)
    most = max(sizes.values())
    return pl.pallas_call(
        functools.partial(xfer_kernel, plan, sizes),
        out_shape=[jax.ShapeDtypeStruct(s, a.dtype) for s, a in zip(dst_shapes, srcs)],
        in_specs=[pl.BlockSpec(memory_space=pl.ANY)] * count,
        out_specs=[pl.BlockSpec(memory_space=pl.ANY)] * count,
        scratch_shapes=[
            pltpu.SemaphoreType.DMA((count, most)),
            pltpu.SemaphoreType.DMA((count, most)),
            pltpu.SemaphoreType.DMA((count,)),
        ],
        compiler_params=pltpu.CompilerParams(has_side_effects=True),
    )(*srcs)


def per_device(tokens, routes, gates, grad_out, w_gate, w_up, w_down):
    experts = lax.axis_size("expert")
    groups = lax.axis_size("dp")
    sizes = {"dp": groups, "expert": experts}
    count = tokens.shape[0]
    width = tokens.shape[1]
    top = routes.shape[1]
    cap = 3 * count * top // (2 * experts)
    slots = experts * cap
    routed = count * top
    flat = routes.reshape(routed)
    labels = jnp.arange(experts, dtype=jnp.int32)
    onehot = (flat[:, None] == labels[None, :]).astype(jnp.int32)
    rank = jnp.sum((jnp.cumsum(onehot, axis=0) - onehot) * onehot, axis=1)
    position = flat * cap + rank
    owner = (
        jnp.full((slots,), routed, jnp.int32).at[position].set(jnp.arange(routed, dtype=jnp.int32))
    )
    source = owner // top
    padded_tokens = jnp.concatenate([tokens, jnp.zeros((1, width), tokens.dtype)], axis=0)
    padded_grads = jnp.concatenate([grad_out, jnp.zeros((1, width), grad_out.dtype)], axis=0)
    padded_gates = jnp.concatenate([gates.reshape(routed), jnp.zeros((1,), jnp.float32)], axis=0)
    inputs_out = padded_tokens[source].reshape(experts, cap, width)
    scaled_out = (padded_gates[owner][:, None] * padded_grads[source].astype(jnp.float32)).astype(
        jnp.bfloat16
    )
    scaled_out = scaled_out.reshape(experts, cap, width)
    share = w_gate.shape[1]
    hid = w_gate.shape[2]
    x_in, s_in, gate_all, up_all, down_all = exchange(
        (("a2a", "expert"), ("a2a", "expert"), ("gather", "dp"), ("gather", "dp"), ("gather", "dp")),
        sizes,
        (inputs_out, scaled_out, w_gate[0], w_up[0], w_down[0]),
        (
            (experts, cap, width),
            (experts, cap, width),
            (groups, share, hid),
            (groups, share, hid),
            (groups, hid, share),
        ),
    )
    x_rows = x_in.reshape(slots, width)
    scaled_rows = s_in.reshape(slots, width)
    gate_full = gate_all.reshape(groups * share, hid)
    up_full = up_all.reshape(groups * share, hid)
    pre_gate = jnp.dot(x_rows, gate_full, preferred_element_type=jnp.float32)
    pre_up = jnp.dot(x_rows, up_full, preferred_element_type=jnp.float32)
    act, slope = silu_parts(pre_gate)
    hidden_f = act * pre_up
    back = jnp.einsum(
        "sgk,ghk->sh",
        scaled_rows.reshape(slots, groups, share),
        down_all,
        preferred_element_type=jnp.float32,
    )
    score = jnp.sum(back * hidden_f, axis=1).astype(jnp.bfloat16)
    d_gate = (back * pre_up * slope).astype(jnp.bfloat16)
    d_up = (back * act).astype(jnp.bfloat16)
    route_grad = (contract_last(d_gate, gate_full) + contract_last(d_up, up_full)).astype(
        jnp.bfloat16
    )
    hidden = hidden_f.astype(jnp.bfloat16)
    partial = jnp.einsum(
        "sh,sgk->ghk",
        hidden,
        scaled_rows.reshape(slots, groups, share),
        preferred_element_type=jnp.float32,
    ).astype(jnp.bfloat16)
    score_box = jnp.zeros((experts, 8, 128), jnp.bfloat16).at[:, 0, :cap].set(
        score.reshape(experts, cap)
    )
    rg_back, score_back, parts_in = exchange(
        (("a2a", "expert"), ("a2a", "expert"), ("a2a", "dp")),
        sizes,
        (route_grad.reshape(experts, cap, width), score_box, partial),
        ((experts, cap, width), (experts, 8, 128), (groups, hid, share)),
    )
    grad_down = jnp.sum(parts_in.astype(jnp.float32), axis=0)[None]
    back_rows = rg_back.reshape(slots, width)
    back_scores = score_back[:, 0, :cap].reshape(slots)
    per_route = back_rows[position].reshape(count, top, width)
    grad_tokens = jnp.sum(per_route.astype(jnp.float32), axis=1).astype(jnp.bfloat16)
    grad_gates = back_scores[position].astype(jnp.float32).reshape(count, top) / gates
    return (grad_tokens, grad_gates, grad_down)


def solution(mesh):
    placed = (
        P(("dp", "expert"), None),
        P(("dp", "expert"), None),
        P(("dp", "expert"), None),
        P(("dp", "expert"), None),
        P("expert", "dp", None),
        P("expert", "dp", None),
        P("expert", None, "dp"),
    )
    return jax.shard_map(
        per_device,
        mesh=mesh,
        in_specs=placed,
        out_specs=(P(("dp", "expert"), None), P(("dp", "expert"), None), P("expert", None, "dp")),
        check_vma=False,
    )
```

time: 453 us -> 411 us (0.907)
  Pallas kernels: 0 us -> 345 us
  waiting for transfers between devices: 318 us -> 0 us
  starting transfers between devices: 50.9 us -> 0 us
  between operations: 14.1 us -> 0.93 us
  matrix products: 21.5 us -> 16.9 us
    pallas_call x0 -> x2, Pallas kernels: none -> 345 us  [exchange(): pl.pallas_call(functools.partial(xfer_kernel, plan, sizes), out_shape=[ja...]
    all_to_all x4 -> x0, waiting for transfers between devices: 289 us -> none  [the longest x1 96.5 us: per_device(): lax.all_to_all(inputs_out, 'expert', split_axis=0, concat_axis=0, tiled=T...]
    all_to_all x4 -> x0, starting transfers between devices: 50.6 us -> none  [the longest x1 19.7 us: per_device(): lax.all_to_all(scaled_out, 'expert', split_axis=0, concat_axis=0, tiled=T...]
    all_gather x3 -> x0, waiting for transfers between devices: 26.6 us -> none  [the longest x1 26.6 us: full_weights(): down_full = lax.all_gather(w_down, 'dp', axis=2, tiled=True)[0]]
    dot_general x3 -> x2, matrix products: 10.1 us -> 2.99 us  [contract_last(): lax.dot_general(left, right, (((1,), (1,)), ((), ())), preferred_element_...]
    another operation x1 -> x5, local copies, waits for them, and re-layouts: 0.01 us -> 5.03 us  [the longest x2 4.7 us: per_device(): scaled_rows.reshape(slots, groups, share)]
    dot_general x3 -> x4, matrix products: 11.4 us -> 13.9 us  [the longest x1 5.34 us: per_device(): jnp.einsum('sh,sgk->ghk', hidden, scaled_rows.reshape(slots, groups, shar...]
  transfers between devices with their start and end apart: 8 -> 0, of which waited for: 5 -> 0; matrix products, arithmetic and copies ran while one was open for 13% -> 0% of each run, Pallas kernels for 0% -> 0%
where the time goes in v1:
time: 411 us; the launch traced here: 410 us
  Pallas kernels  345 us (84%)
  local copies, waits for them, and re-layouts  34.8 us (8%)
  matrix products  16.9 us (4%)
  other arithmetic  12.5 us (3%)
    pallas_call x2, Pallas kernels, exchange(): pl.pallas_call(functools.partial(xfer_kernel, plan, sizes), out_shape=[ja...  345 us

profile of v1, /device:TPU:1, one launch (start us, length us, event | category | flops | bytes accessed | tf_op | source)
XLA Modules:
  0.0 410.1 jit_solution(13421538002404070833)
XLA Ops:
  0.6 0.8 copy.14
  1.4 0.1 eq.29
  1.6 0.6 reduce-window.6
  2.2 0.2 slice_reduce_fusion
  2.4 0.1 eq.25
  2.6 0.1 fusion.8
  2.7 0.7 broadcast_multiply_fusion
  3.4 0.1 copy.13
  3.5 0.1 mul.56
  3.6 1.4 scatter_custom_fusion
  5.1 1.1 concatenate.13
  6.2 2.5 gather_fusion.2
  8.6 0.0 copy-start.1
  8.6 2.1 reshape.149
  10.8 0.0 copy-done.1
  10.8 0.1 copy.17
  10.9 0.1 reshape.142
  11.0 2.8 gather_fusion.1
  13.9 0.1 mul.58
  14.0 0.0 copy-start
  14.0 4.0 multiply_convert_fusion.refs_1_
  18.0 0.0 copy-done
  18.0 2.5 gather_fusion
  20.5 1.6 reshape.141.refs_0_
  22.1 212.4 %shard_map.94 = (bf16[64,6,2048]{2,1,0:T(8,128)(2,1)}, bf16[64,6,2048]{2,1,0:T(8,128)(2,1)}, bf16[8,256,768]{2,1,0:T(8,128)(2,1)}, bf16[8,256,768]{2,1,0:T(8,128)(2,1)}, bf16[8,768,256]{2,1,0:T(8,128)(2,1)}) custom-call(bf16[64,6,2048]{2,1,0:T(8,128)(2,1)} %reshape.141.refs_0_, bf16[64,6,2048]{2,1,0:T(8,128)(2,1)} %multiply_convert_fusion.refs_1_, ...), custom_call_target="tpu_custom_call" | custom-call | tf_op jit(solution)/shard_map/pallas_call | solution.py:75
  234.4 2.6 reshape.143
  237.1 0.0 copy-start.3
  237.1 4.5 %fusion.17 = f32[384,768]{1,0:T(8,128)} fusion(bf16[384,2048]{1,0:T(8,128)(2,1)S(1)} %reshape.143, bf16[2048,768]{1,0:T(8,128)(2,1)} %bitcast.50), kind=kOutput, calls=%fused_computation.49 | convolution fusion | flops 1207959552 | bytes 5898240 | tf_op jit(solution)/shard_map/dot_general | solution.py:135
  241.6 0.0 copy-done.3
  241.6 2.4 fusion.18
  244.0 3.4 reshape_reshape.4
  247.4 1.3 copy.20
  248.7 0.0 copy-start.5
  248.7 0.0 copy-start.6
  248.7 0.0 copy-start.7
  248.7 5.3 %convert_bitcast_fusion.refs_2_ = bf16[8,768,256]{2,1,0:T(8,128)(2,1)} fusion(bf16[384,8,256]{0,2,1:T(8,128)(2,1)S(1)} %copy.20, f32[384,768]{1,0:T(8,128)} %fusion.17, f32[384,768]{1,0:T(8,128)} %fusion.18), kind=kOutput, calls=%fused_computation.8 | convolution fusion | flops 1211301888 | bytes 7077888 | tf_op jit(solution)/shard_map/sh,sgk->ghk/dot_general | solution.py:151
  254.1 0.0 copy-done.5
  254.1 0.0 copy-done.6
  254.1 0.0 copy-done.7
  254.1 0.0 copy-start.4
  254.1 1.6 multiply_reduce_fusion
  255.7 0.2 copy-done.4
  256.0 0.0 copy-start.2
  256.0 1.6 fusion.1
  257.6 0.3 copy-done.2
  257.9 1.4 add_convert_fusion
  259.3 1.6 reshape.146.refs_0_
  261.0 0.2 convert_element_type.79
  261.1 0.7 scatter.13.refs_1_
  261.8 132.6 %shard_map.95 = (bf16[64,6,2048]{2,1,0:T(8,128)(2,1)}, bf16[64,8,128]{2,1,0:T(8,128)(2,1)}, bf16[8,768,256]{2,1,0:T(8,128)(2,1)}) custom-call(bf16[64,6,2048]{2,1,0:T(8,128)(2,1)} %reshape.146.refs_0_, bf16[64,8,128]{2,1,0:T(8,128)(2,1)} %scatter.13.refs_1_, bf16[8,768,256]{2,1,0:T(8,128)(2,1)} %convert_bitcast_fusion.refs_2_), custom_call_target="tpu_custom_call" | custom-call | tf_op jit(solution)/shard_map/pallas_call | solution.py:75
  394.4 2.6 reshape.147
  397.1 1.4 gather_fusion.3
  398.4 0.7 reshape.148
  399.2 3.8 reduce_sum.44
  402.9 3.3 convert_reduce_fusion
  406.2 1.0 slice_reduce_fusion.1
  407.2 0.1 reshape_squeeze.3
  407.4 1.9 gather_fusion.4
  409.3 0.1 reshape.150
  409.5 0.6 copy.23
  (11 shorter events, 0.2 us)
Async XLA Ops:
  8.6 2.2 copy-start.1
  14.0 4.0 copy-start
  237.1 4.5 %copy-start.3 = (bf16[8,256,768]{2,1,0:T(8,128)(2,1)S(1)}, bf16[8,256,768]{2,1,0:T(8,128)(2,1)}, u32[]{:S(2)}) copy-start(bf16[8,256,768]{2,1,0:T(8,128)(2,1)} %get-tuple-element.27) | copy-start | bytes 9437188
  248.7 5.4 %copy-start.5 = (bf16[8,768,256]{2,1,0:T(8,128)(2,1)S(1)}, bf16[8,768,256]{2,1,0:T(8,128)(2,1)}, u32[]{:S(2)}) copy-start(bf16[8,768,256]{2,1,0:T(8,128)(2,1)} %get-tuple-element.24) | copy-start | bytes 9437188
  248.7 5.4 %copy-start.6 = (f32[384,768]{1,0:T(8,128)S(1)}, f32[384,768]{1,0:T(8,128)}, u32[]{:S(2)}) copy-start(f32[384,768]{1,0:T(8,128)} %fusion.18) | copy-start | bytes 3538948
  248.7 5.4 %copy-start.7 = (f32[384,768]{1,0:T(8,128)S(1)}, f32[384,768]{1,0:T(8,128)}, u32[]{:S(2)}) copy-start(f32[384,768]{1,0:T(8,128)} %fusion.17) | copy-start | bytes 3538948
  254.1 1.9 copy-start.4
  256.0 1.9 copy-start.2

commit v2 on v1

--- a/solution.py
+++ b/solution.py
@@ -108,11 +108,12 @@
     padded_tokens = jnp.concatenate([tokens, jnp.zeros((1, width), tokens.dtype)], axis=0)
     padded_grads = jnp.concatenate([grad_out, jnp.zeros((1, width), grad_out.dtype)], axis=0)
     padded_gates = jnp.concatenate([gates.reshape(routed), jnp.zeros((1,), jnp.float32)], axis=0)
-    inputs_out = padded_tokens[source].reshape(experts, cap, width)
+    dense = (experts, cap * width // 128, 128)
+    inputs_out = padded_tokens[source].reshape(dense)
     scaled_out = (padded_gates[owner][:, None] * padded_grads[source].astype(jnp.float32)).astype(
         jnp.bfloat16
     )
-    scaled_out = scaled_out.reshape(experts, cap, width)
+    scaled_out = scaled_out.reshape(dense)
     share = w_gate.shape[1]
     hid = w_gate.shape[2]
     x_in, s_in, gate_all, up_all, down_all = exchange(
@@ -120,8 +121,8 @@
         sizes,
         (inputs_out, scaled_out, w_gate[0], w_up[0], w_down[0]),
         (
-            (experts, cap, width),
-            (experts, cap, width),
+            dense,
+            dense,
             (groups, share, hid),
             (groups, share, hid),
             (groups, hid, share),
@@ -160,8 +161,8 @@
     rg_back, score_back, parts_in = exchange(
         (("a2a", "expert"), ("a2a", "expert"), ("a2a", "dp")),
         sizes,
-        (route_grad.reshape(experts, cap, width), score_box, partial),
-        ((experts, cap, width), (experts, 8, 128), (groups, hid, share)),
+        (route_grad.reshape(dense), score_box, partial),
+        (dense, (experts, 8, 128), (groups, hid, share)),
     )
     grad_down = jnp.sum(parts_in.astype(jnp.float32), axis=0)[None]
     back_rows = rg_back.reshape(slots, width)

time: 411 us -> 342 us (0.83)
  Pallas kernels: 345 us -> 277 us
    pallas_call x2, Pallas kernels: 345 us -> 277 us  [exchange(): pl.pallas_call(functools.partial(xfer_kernel, plan, sizes), out_shape=[ja...]
where the time goes in v2:
time: 342 us
  Pallas kernels  277 us (81%)
  local copies, waits for them, and re-layouts  33.8 us (10%)
  matrix products  19.4 us (6%)
  other arithmetic  10.3 us (3%)
    pallas_call x2, Pallas kernels, exchange(): pl.pallas_call(functools.partial(xfer_kernel, plan, sizes), out_shape=[ja...  277 us

profile of v2, /device:TPU:1, one launch (start us, length us, event | category | flops | bytes accessed | tf_op | source)
XLA Modules:
  0.0 341.7 jit_solution(6321772499348023235)
XLA Ops:
  0.6 1.1 concatenate.11
  1.7 0.7 broadcast_multiply_fusion
  2.4 0.1 copy.13
  2.5 0.1 mul.60
  2.7 0.8 copy.14
  3.5 0.1 eq.25
  3.6 0.1 eq.29
  3.7 0.6 reduce-window.6
  4.4 0.2 slice_reduce_fusion
  4.6 0.1 fusion.8
  4.7 1.4 scatter_custom_fusion
  6.2 2.5 gather_fusion
  8.6 0.0 copy-start.1
  8.6 2.1 reshape.139.refs_0_
  10.8 0.0 copy-done.1
  10.8 3.1 gather_fusion.2
  13.9 0.0 copy-start.2
  13.9 2.5 reshape.147
  16.5 0.0 copy-done.2
  16.5 0.1 copy.17
  16.6 0.1 reshape.140
  16.8 2.8 gather_fusion.1
  19.6 0.1 mul.62
  19.7 0.1 copy.18
  19.8 0.1 copy.19
  19.9 1.9 multiply_convert_fusion.refs_1_
  21.7 167.8 %shard_map.94 = (bf16[64,96,128]{2,1,0:T(8,128)(2,1)}, bf16[64,96,128]{2,1,0:T(8,128)(2,1)}, bf16[8,256,768]{2,1,0:T(8,128)(2,1)}, bf16[8,256,768]{2,1,0:T(8,128)(2,1)}, bf16[8,768,256]{2,1,0:T(8,128)(2,1)}) custom-call(bf16[64,96,128]{2,1,0:T(8,128)(2,1)} %reshape.139.refs_0_, bf16[64,96,128]{2,1,0:T(8,128)(2,1)} %multiply_convert_fusion.refs_1_, ...), custom_call_target="tpu_custom_call" | custom-call | tf_op jit(solution)/shard_map/pallas_call | solution.py:75
  189.5 2.5 reshape.141
  192.1 0.0 copy-start.3
  192.1 4.4 %fusion.18 = f32[384,768]{1,0:T(8,128)} fusion(bf16[384,2048]{1,0:T(8,128)(2,1)S(1)} %reshape.141, bf16[2048,768]{1,0:T(8,128)(2,1)} %bitcast.54), kind=kOutput, calls=%fused_computation.50 | convolution fusion | flops 1207959552 | bytes 5898240 | tf_op jit(solution)/shard_map/dot_general | solution.py:135
  196.5 0.0 copy-done.3
  196.5 0.0 copy-start
  196.5 2.5 fusion.17
  199.0 0.0 copy-done
  199.0 0.6 reshape_reshape.4
  199.6 1.3 copy.22
  200.9 0.0 copy-start.5
  200.9 0.0 copy-start.6
  200.9 0.0 copy-start.7
  200.9 4.3 %multiply_reduce_fusion = (bf16[384]{0:T(512)(128)(2,1)S(1)}, f32[384,768]{1,0:T(8,128)S(1)}) fusion(f32[384,768]{1,0:T(8,128)} %fusion.17, f32[384,768]{1,0:T(8,128)} %fusion.18, bf16[384,8,256]{0,2,1:T(8,128)(2,1)S(1)} %copy.22, bf16[8,768,256]{2,1,0:T(8,128)(2,1)} %get-tuple-element.24), kind=kOutput, calls=%fused_computation.11 | convolution fusion | flops 1210023552 | bytes 8258304 | tf_op jit(solution)/shard_map/sgk,ghk->sh/dot_general | solution.py:139
  205.2 0.0 copy-done.5
  205.2 0.0 copy-done.6
  205.2 0.0 copy-done.7
  205.2 0.0 copy-start.4
  205.2 1.6 fusion.1
  206.8 0.3 copy-done.4
  207.1 1.4 add_convert_fusion
  208.6 2.1 reshape.144.refs_0_
  210.7 0.2 convert_element_type.79
  210.8 0.7 scatter.13.refs_1_
  211.5 5.2 %convert_bitcast_fusion.refs_2_ = bf16[8,768,256]{2,1,0:T(8,128)(2,1)} fusion(bf16[384,8,256]{0,2,1:T(8,128)(2,1)S(1)} %copy.22, f32[384,768]{1,0:T(8,128)} %fusion.17, f32[384,768]{1,0:T(8,128)} %fusion.18), kind=kOutput, calls=%fused_computation.7 | convolution fusion | flops 1211301888 | bytes 7077888 | tf_op jit(solution)/shard_map/sh,sgk->ghk/dot_general | solution.py:152
  216.7 109.5 %shard_map.95 = (bf16[64,96,128]{2,1,0:T(8,128)(2,1)}, bf16[64,8,128]{2,1,0:T(8,128)(2,1)}, bf16[8,768,256]{2,1,0:T(8,128)(2,1)}) custom-call(bf16[64,96,128]{2,1,0:T(8,128)(2,1)} %reshape.144.refs_0_, bf16[64,8,128]{2,1,0:T(8,128)(2,1)} %scatter.13.refs_1_, bf16[8,768,256]{2,1,0:T(8,128)(2,1)} %convert_bitcast_fusion.refs_2_), custom_call_target="tpu_custom_call" | custom-call | tf_op jit(solution)/shard_map/pallas_call | solution.py:75
  326.2 2.5 reshape.145
  328.8 1.4 gather_fusion.3
  330.1 0.7 reshape.146
  330.9 3.6 %reduce_sum.44 = bf16[128,2048]{1,0:T(8,128)(2,1)} reduce(bf16[128,2,2048]{2,1,0:T(2,128)(2,1)S(1)} %reshape.146, bf16[]{:T(256)} %constant.57.clone.1), dimensions={1}, to_apply=%region_5.6 | reduce | flops 262144 | bytes 1572866 | tf_op jit(solution)/shard_map/reduce_sum | solution.py:171
  334.5 1.0 slice_reduce_fusion.1
  335.5 0.1 reshape_squeeze.3
  335.6 1.9 gather_fusion.4
  337.6 0.1 reshape.148
  337.8 0.6 copy.25
  338.4 3.3 convert_reduce_fusion
  (12 shorter events, 0.2 us)
Async XLA Ops:
  8.6 2.1 copy-start.1
  13.9 2.5 copy-start.2
  192.1 4.4 %copy-start.3 = (bf16[8,256,768]{2,1,0:T(8,128)(2,1)S(1)}, bf16[8,256,768]{2,1,0:T(8,128)(2,1)}, u32[]{:S(2)}) copy-start(bf16[8,256,768]{2,1,0:T(8,128)(2,1)} %get-tuple-element.26) | copy-start | bytes 9437188
  196.5 2.5 copy-start
  200.9 4.3 %copy-start.5 = (bf16[8,256,768]{2,1,0:T(8,128)(2,1)S(1)}, bf16[8,256,768]{2,1,0:T(8,128)(2,1)}, u32[]{:S(2)}) copy-start(bf16[8,256,768]{2,1,0:T(8,128)(2,1)} %get-tuple-element.27) | copy-start | bytes 9437188
  200.9 4.3 %copy-start.6 = (f32[384,768]{1,0:T(8,128)S(1)}, f32[384,768]{1,0:T(8,128)}, u32[]{:S(2)}) copy-start(f32[384,768]{1,0:T(8,128)} %fusion.18) | copy-start | bytes 3538948
  200.9 4.3 %copy-start.7 = (f32[384,768]{1,0:T(8,128)S(1)}, f32[384,768]{1,0:T(8,128)}, u32[]{:S(2)}) copy-start(f32[384,768]{1,0:T(8,128)} %fusion.17) | copy-start | bytes 3538948
  205.2 1.9 copy-start.4

commit v3 on v2

--- a/solution.py
+++ b/solution.py
@@ -17,6 +17,11 @@
     return lax.dot_general(
         left, right, (((1,), (1,)), ((), ())), preferred_element_type=jnp.float32
     )
+
+
+def turn(j, n):
+    odd = j % 2
+    return odd * ((j + 1) // 2) + (1 - odd) * (n - j // 2)
 
 
 def xfer_kernel(plan, sizes, *refs):
@@ -42,6 +47,21 @@
             device_id_type=pl.DeviceIdType.MESH,
         )
 
+    barrier = pltpu.get_barrier_semaphore()
+    axes = sorted(set(axis for _, axis in plan))
+    for axis in axes:
+        me, n = mine[axis], sizes[axis]
+
+        @pl.loop(1, n)
+        def _(j):
+            peer = lax.rem(me + j, n)
+            device = (peer, me_ex) if axis == "dp" else (me_dp, peer)
+            pl.semaphore_signal(
+                barrier, 1, device_id=device, device_id_type=pl.DeviceIdType.MESH
+            )
+
+    pl.semaphore_wait(barrier, sum(sizes[axis] - 1 for axis in axes))
+
     local = []
     for i, (kind, axis) in enumerate(plan):
         me = mine[axis]
@@ -53,7 +73,7 @@
 
         @pl.loop(1, n)
         def _(j):
-            peer = lax.rem(me + j, n)
+            peer = lax.rem(me + turn(j, n), n)
             remote(i, peer, me).start()
 
     for i, (kind, axis) in enumerate(plan):
@@ -61,7 +81,7 @@
 
         @pl.loop(1, n)
         def _(j):
-            peer = lax.rem(me + j, n)
+            peer = lax.rem(me + turn(j, n), n)
             remote(i, peer, me).wait_send()
             remote(i, peer, peer).wait_recv()
 
@@ -69,7 +89,7 @@
         copy.wait()
 
 
-def exchange(plan, sizes, srcs, dst_shapes):
+def exchange(plan, sizes, srcs, dst_shapes, tag):
     count = len(plan)
     most = max(sizes.values())
     return pl.pallas_call(
@@ -82,7 +102,7 @@
             pltpu.SemaphoreType.DMA((count, most)),
             pltpu.SemaphoreType.DMA((count,)),
         ],
-        compiler_params=pltpu.CompilerParams(has_side_effects=True),
+        compiler_params=pltpu.CompilerParams(collective_id=tag, has_side_effects=True),
     )(*srcs)
 
 
@@ -127,6 +147,7 @@
             (groups, share, hid),
             (groups, hid, share),
         ),
+        0,
     )
     x_rows = x_in.reshape(slots, width)
     scaled_rows = s_in.reshape(slots, width)
@@ -163,6 +184,7 @@
         sizes,
         (route_grad.reshape(dense), score_box, partial),
         (dense, (experts, 8, 128), (groups, hid, share)),
+        1,
     )
     grad_down = jnp.sum(parts_in.astype(jnp.float32), axis=0)[None]
     back_rows = rg_back.reshape(slots, width)

time: 342 us -> 321 us (0.939)
  Pallas kernels: 277 us -> 255 us
    pallas_call x2, Pallas kernels: 277 us -> 255 us  [exchange(): pl.pallas_call(functools.partial(xfer_kernel, plan, sizes), out_shape=[ja...]
where the time goes in v3:
time: 321 us; the launch traced here: 319 us
  Pallas kernels  255 us (79%)
  local copies, waits for them, and re-layouts  33.9 us (11%)
  matrix products  19.4 us (6%)
  other arithmetic  10.3 us (3%)
    pallas_call x2, Pallas kernels, exchange(): pl.pallas_call(functools.partial(xfer_kernel, plan, sizes), out_shape=[ja...  255 us

profile of v3, /device:TPU:1, one launch (start us, length us, event | category | flops | bytes accessed | tf_op | source)
XLA Modules:
  0.0 319.4 jit_solution(18291568869030442851)
XLA Ops:
  0.6 1.1 concatenate.11
  1.7 0.7 broadcast_multiply_fusion
  2.4 0.1 copy.13
  2.5 0.1 mul.60
  2.7 0.8 copy.14
  3.5 0.1 eq.25
  3.6 0.1 eq.29
  3.7 0.6 reduce-window.6
  4.4 0.2 slice_reduce_fusion
  4.6 0.1 fusion.8
  4.7 1.4 scatter_custom_fusion
  6.2 2.5 gather_fusion
  8.6 0.0 copy-start.1
  8.6 2.1 reshape.139.refs_0_
  10.8 0.0 copy-done.1
  10.8 3.1 gather_fusion.2
  13.9 0.0 copy-start.2
  13.9 2.5 reshape.147
  16.5 0.0 copy-done.2
  16.5 0.1 copy.17
  16.6 0.1 reshape.140
  16.8 2.8 gather_fusion.1
  19.6 0.1 mul.62
  19.7 0.1 copy.18
  19.8 0.1 copy.19
  19.9 1.9 multiply_convert_fusion.refs_1_
  21.7 162.5 %shard_map.94 = (bf16[64,96,128]{2,1,0:T(8,128)(2,1)}, bf16[64,96,128]{2,1,0:T(8,128)(2,1)}, bf16[8,256,768]{2,1,0:T(8,128)(2,1)}, bf16[8,256,768]{2,1,0:T(8,128)(2,1)}, bf16[8,768,256]{2,1,0:T(8,128)(2,1)}) custom-call(bf16[64,96,128]{2,1,0:T(8,128)(2,1)} %reshape.139.refs_0_, bf16[64,96,128]{2,1,0:T(8,128)(2,1)} %multiply_convert_fusion.refs_1_, ...), custom_call_target="tpu_custom_call" | custom-call | tf_op jit(solution)/shard_map/pallas_call | solution.py:95
  184.3 2.5 reshape.141
  186.8 0.0 copy-start.3
  186.8 4.4 %fusion.18 = f32[384,768]{1,0:T(8,128)} fusion(bf16[384,2048]{1,0:T(8,128)(2,1)S(1)} %reshape.141, bf16[2048,768]{1,0:T(8,128)(2,1)} %bitcast.54), kind=kOutput, calls=%fused_computation.50 | convolution fusion | flops 1207959552 | bytes 5898240 | tf_op jit(solution)/shard_map/dot_general | solution.py:156
  191.3 0.0 copy-done.3
  191.3 0.0 copy-start
  191.3 2.5 fusion.17
  193.8 0.0 copy-done
  193.8 0.6 reshape_reshape.4
  194.3 1.4 copy.22
  195.8 0.0 copy-start.5
  195.8 0.0 copy-start.6
  195.8 0.0 copy-start.7
  195.8 4.3 %multiply_reduce_fusion = (bf16[384]{0:T(512)(128)(2,1)S(1)}, f32[384,768]{1,0:T(8,128)S(1)}) fusion(f32[384,768]{1,0:T(8,128)} %fusion.17, f32[384,768]{1,0:T(8,128)} %fusion.18, bf16[384,8,256]{0,2,1:T(8,128)(2,1)S(1)} %copy.22, bf16[8,768,256]{2,1,0:T(8,128)(2,1)} %get-tuple-element.24), kind=kOutput, calls=%fused_computation.11 | convolution fusion | flops 1210023552 | bytes 8258304 | tf_op jit(solution)/shard_map/sgk,ghk->sh/dot_general | solution.py:160
  200.1 0.0 copy-done.5
  200.1 0.0 copy-done.6
  200.2 0.0 copy-done.7
  200.2 0.0 copy-start.4
  200.2 1.6 fusion.1
  201.7 0.3 copy-done.4
  202.1 1.4 add_convert_fusion
  203.5 2.1 reshape.144.refs_0_
  205.6 0.2 convert_element_type.79
  205.8 0.7 scatter.13.refs_1_
  206.5 5.2 %convert_bitcast_fusion.refs_2_ = bf16[8,768,256]{2,1,0:T(8,128)(2,1)} fusion(bf16[384,8,256]{0,2,1:T(8,128)(2,1)S(1)} %copy.22, f32[384,768]{1,0:T(8,128)} %fusion.17, f32[384,768]{1,0:T(8,128)} %fusion.18), kind=kOutput, calls=%fused_computation.7 | convolution fusion | flops 1211301888 | bytes 7077888 | tf_op jit(solution)/shard_map/sh,sgk->ghk/dot_general | solution.py:173
  211.7 92.2 %shard_map.95 = (bf16[64,96,128]{2,1,0:T(8,128)(2,1)}, bf16[64,8,128]{2,1,0:T(8,128)(2,1)}, bf16[8,768,256]{2,1,0:T(8,128)(2,1)}) custom-call(bf16[64,96,128]{2,1,0:T(8,128)(2,1)} %reshape.144.refs_0_, bf16[64,8,128]{2,1,0:T(8,128)(2,1)} %scatter.13.refs_1_, bf16[8,768,256]{2,1,0:T(8,128)(2,1)} %convert_bitcast_fusion.refs_2_), custom_call_target="tpu_custom_call" | custom-call | tf_op jit(solution)/shard_map/pallas_call | solution.py:95
  303.9 2.5 reshape.145
  306.5 1.4 gather_fusion.3
  307.9 0.7 reshape.146
  308.6 3.6 %reduce_sum.44 = bf16[128,2048]{1,0:T(8,128)(2,1)} reduce(bf16[128,2,2048]{2,1,0:T(2,128)(2,1)S(1)} %reshape.146, bf16[]{:T(256)} %constant.57.clone.1), dimensions={1}, to_apply=%region_5.6 | reduce | flops 262144 | bytes 1572866 | tf_op jit(solution)/shard_map/reduce_sum | solution.py:193
  312.2 1.0 slice_reduce_fusion.1
  313.2 0.1 reshape_squeeze.3
  313.4 1.9 gather_fusion.4
  315.3 0.1 reshape.148
  315.5 0.6 copy.25
  316.1 3.3 %convert_reduce_fusion = f32[768,256]{1,0:T(8,128)} fusion(bf16[8,768,256]{2,1,0:T(8,128)(2,1)} %get-tuple-element.30), kind=kLoop, calls=%fused_computation.6 | loop fusion | flops 2949120 | bytes 3932160 | tf_op jit(solution)/shard_map/reduce_sum | solution.py:189
  (12 shorter events, 0.2 us)
Async XLA Ops:
  8.6 2.1 copy-start.1
  13.9 2.5 copy-start.2
  186.8 4.4 %copy-start.3 = (bf16[8,256,768]{2,1,0:T(8,128)(2,1)S(1)}, bf16[8,256,768]{2,1,0:T(8,128)(2,1)}, u32[]{:S(2)}) copy-start(bf16[8,256,768]{2,1,0:T(8,128)(2,1)} %get-tuple-element.26) | copy-start | bytes 9437188
  191.3 2.5 copy-start
  195.8 4.3 %copy-start.5 = (bf16[8,256,768]{2,1,0:T(8,128)(2,1)S(1)}, bf16[8,256,768]{2,1,0:T(8,128)(2,1)}, u32[]{:S(2)}) copy-start(bf16[8,256,768]{2,1,0:T(8,128)(2,1)} %get-tuple-element.27) | copy-start | bytes 9437188
  195.8 4.3 %copy-start.6 = (f32[384,768]{1,0:T(8,128)S(1)}, f32[384,768]{1,0:T(8,128)}, u32[]{:S(2)}) copy-start(f32[384,768]{1,0:T(8,128)} %fusion.18) | copy-start | bytes 3538948
  195.8 4.3 %copy-start.7 = (f32[384,768]{1,0:T(8,128)S(1)}, f32[384,768]{1,0:T(8,128)}, u32[]{:S(2)}) copy-start(f32[384,768]{1,0:T(8,128)} %fusion.17) | copy-start | bytes 3538948
  200.2 1.9 copy-start.4

commit v4 on v3

--- a/solution.py
+++ b/solution.py
@@ -125,56 +125,49 @@
         jnp.full((slots,), routed, jnp.int32).at[position].set(jnp.arange(routed, dtype=jnp.int32))
     )
     source = owner // top
-    padded_tokens = jnp.concatenate([tokens, jnp.zeros((1, width), tokens.dtype)], axis=0)
-    padded_grads = jnp.concatenate([grad_out, jnp.zeros((1, width), grad_out.dtype)], axis=0)
+    lanes = width // 128
+    pick = (source[:, None] == jnp.arange(count, dtype=jnp.int32)[None, :]).astype(jnp.bfloat16)
+    select = (((1,), (0,)), ((), ()))
+    x_send = lax.dot_general(
+        pick, tokens.reshape(count, lanes, 128), select, preferred_element_type=jnp.float32
+    ).astype(jnp.bfloat16)
+    g_rows = lax.dot_general(
+        pick, grad_out.reshape(count, lanes, 128), select, preferred_element_type=jnp.float32
+    )
     padded_gates = jnp.concatenate([gates.reshape(routed), jnp.zeros((1,), jnp.float32)], axis=0)
-    dense = (experts, cap * width // 128, 128)
-    inputs_out = padded_tokens[source].reshape(dense)
-    scaled_out = (padded_gates[owner][:, None] * padded_grads[source].astype(jnp.float32)).astype(
-        jnp.bfloat16
-    )
-    scaled_out = scaled_out.reshape(dense)
+    s_send = (padded_gates[owner][:, None, None] * g_rows).astype(jnp.bfloat16)
+    dense = (experts, cap * lanes, 128)
     share = w_gate.shape[1]
     hid = w_gate.shape[2]
     x_in, s_in, gate_all, up_all, down_all = exchange(
         (("a2a", "expert"), ("a2a", "expert"), ("gather", "dp"), ("gather", "dp"), ("gather", "dp")),
         sizes,
-        (inputs_out, scaled_out, w_gate[0], w_up[0], w_down[0]),
-        (
-            dense,
-            dense,
-            (groups, share, hid),
-            (groups, share, hid),
-            (groups, hid, share),
-        ),
+        (x_send.reshape(dense), s_send.reshape(dense), w_gate[0], w_up[0], w_down[0].T),
+        (dense, dense, (groups, share, hid), (groups, share, hid), (groups, share, hid)),
         0,
     )
-    x_rows = x_in.reshape(slots, width)
-    scaled_rows = s_in.reshape(slots, width)
-    gate_full = gate_all.reshape(groups * share, hid)
-    up_full = up_all.reshape(groups * share, hid)
-    pre_gate = jnp.dot(x_rows, gate_full, preferred_element_type=jnp.float32)
-    pre_up = jnp.dot(x_rows, up_full, preferred_element_type=jnp.float32)
+    x3 = x_in.reshape(slots, lanes, 128)
+    s3 = s_in.reshape(slots, lanes, 128)
+    gate3 = gate_all.reshape(lanes, 128, hid)
+    up3 = up_all.reshape(lanes, 128, hid)
+    down3 = down_all.reshape(lanes, 128, hid)
+    over_d = (((1, 2), (0, 1)), ((), ()))
+    pre_gate = lax.dot_general(x3, gate3, over_d, preferred_element_type=jnp.float32)
+    pre_up = lax.dot_general(x3, up3, over_d, preferred_element_type=jnp.float32)
     act, slope = silu_parts(pre_gate)
     hidden_f = act * pre_up
-    back = jnp.einsum(
-        "sgk,ghk->sh",
-        scaled_rows.reshape(slots, groups, share),
-        down_all,
-        preferred_element_type=jnp.float32,
-    )
+    back = lax.dot_general(s3, down3, over_d, preferred_element_type=jnp.float32)
     score = jnp.sum(back * hidden_f, axis=1).astype(jnp.bfloat16)
     d_gate = (back * pre_up * slope).astype(jnp.bfloat16)
     d_up = (back * act).astype(jnp.bfloat16)
-    route_grad = (contract_last(d_gate, gate_full) + contract_last(d_up, up_full)).astype(
-        jnp.bfloat16
-    )
+    over_h = (((1,), (2,)), ((), ()))
+    route_grad = (
+        lax.dot_general(d_gate, gate3, over_h, preferred_element_type=jnp.float32)
+        + lax.dot_general(d_up, up3, over_h, preferred_element_type=jnp.float32)
+    ).astype(jnp.bfloat16)
     hidden = hidden_f.astype(jnp.bfloat16)
-    partial = jnp.einsum(
-        "sh,sgk->ghk",
-        hidden,
-        scaled_rows.reshape(slots, groups, share),
-        preferred_element_type=jnp.float32,
+    partial = lax.dot_general(
+        s3, hidden, (((0,), (0,)), ((), ())), preferred_element_type=jnp.float32
     ).astype(jnp.bfloat16)
     score_box = jnp.zeros((experts, 8, 128), jnp.bfloat16).at[:, 0, :cap].set(
         score.reshape(experts, cap)
@@ -182,15 +175,17 @@
     rg_back, score_back, parts_in = exchange(
         (("a2a", "expert"), ("a2a", "expert"), ("a2a", "dp")),
         sizes,
-        (route_grad.reshape(dense), score_box, partial),
-        (dense, (experts, 8, 128), (groups, hid, share)),
+        (route_grad.reshape(dense), score_box, partial.reshape(groups, share, hid)),
+        (dense, (experts, 8, 128), (groups, share, hid)),
         1,
     )
-    grad_down = jnp.sum(parts_in.astype(jnp.float32), axis=0)[None]
-    back_rows = rg_back.reshape(slots, width)
+    grad_down = jnp.sum(parts_in.astype(jnp.float32), axis=0).T[None]
+    summed = lax.dot_general(
+        pick, rg_back.reshape(slots, lanes, 128), (((0,), (0,)), ((), ())),
+        preferred_element_type=jnp.float32,
+    )
+    grad_tokens = summed.astype(jnp.bfloat16).reshape(count, width)
     back_scores = score_back[:, 0, :cap].reshape(slots)
-    per_route = back_rows[position].reshape(count, top, width)
-    grad_tokens = jnp.sum(per_route.astype(jnp.float32), axis=1).astype(jnp.bfloat16)
     grad_gates = back_scores[position].astype(jnp.float32).reshape(count, top) / gates
     return (grad_tokens, grad_gates, grad_down)
 

time: 321 us -> 306 us (0.953)
  local copies, waits for them, and re-layouts: 33.9 us -> 25 us
  other arithmetic: 10.3 us -> 4.04 us
    gather x4 -> x1, local copies, waits for them, and re-layouts: 9.74 us -> 2.8 us  [per_device(): s_send = (padded_gates[owner][:, None, None] * g_rows).astype(jnp.bfloat16)]
    reshape x5 -> x2, local copies, waits for them, and re-layouts: 10 us -> 4.4 us  [the longest x1 2.29 us: per_device(): s3 = s_in.reshape(slots, lanes, 128)]
    reduce_sum x2 -> x1, other arithmetic: 6.9 us -> 2.4 us  [per_device(): grad_down = jnp.sum(parts_in.astype(jnp.float32), axis=0).T[None]]
    convert_element_type x1 -> x3, local copies, waits for them, and re-layouts: 2.53 us -> 6.52 us  [the longest x1 2.21 us: per_device(): s_send = (padded_gates[owner][:, None, None] * g_rows).astype(jnp.bfloat16)]
    dot_general x6 -> x8, matrix products: 19.4 us -> 19.5 us  [the longest x1 4.85 us: per_device(): lax.dot_general(s3, hidden, (((0,), (0,)), ((), ())), preferred_element_t...]
where the time goes in v4:
time: 306 us; the launch traced here: 305 us
  Pallas kernels  255 us (83%)
  local copies, waits for them, and re-layouts  25 us (8%)
  matrix products  20.2 us (7%)
  other arithmetic  4.04 us (1%)
    pallas_call x2, Pallas kernels, exchange(): pl.pallas_call(functools.partial(xfer_kernel, plan, sizes), out_shape=[ja...  255 us

profile of v4, /device:TPU:1, one launch (start us, length us, event | category | flops | bytes accessed | tf_op | source)
XLA Modules:
  0.0 304.9 jit_solution(10821534673404927394)
XLA Ops:
  0.6 0.0 copy-start
  0.6 0.7 broadcast_multiply_fusion
  1.4 0.1 copy.42
  1.5 0.1 mul.53
  1.6 0.8 copy.43
  2.4 0.1 eq.38
  2.6 0.1 eq.42
  2.7 0.6 reduce-window.6
  3.3 0.2 slice_reduce_fusion
  3.6 0.1 fusion.23
  3.7 1.4 scatter_custom_fusion
  5.1 0.0 copy-done
  5.1 0.6 convolution_convert_fusion.1
  5.8 0.0 copy-start.3
  5.8 2.1 copy.47
  7.9 0.0 copy-start.1
  7.9 0.0 copy-done.3
  7.9 0.1 copy.48
  8.0 0.1 reshape.153
  8.2 2.8 gather_fusion
  11.0 0.0 copy-done.1
  11.0 0.6 multiply_convert_fusion
  11.6 0.0 copy-start.2
  11.6 2.2 copy.50
  13.9 0.0 copy-done.2
  13.9 0.9 copy.51
  14.8 162.5 %shard_map.94 = (bf16[64,96,128]{2,1,0:T(8,128)(2,1)}, bf16[64,96,128]{2,1,0:T(8,128)(2,1)}, bf16[8,256,768]{2,1,0:T(8,128)(2,1)}, bf16[8,256,768]{2,1,0:T(8,128)(2,1)}, bf16[8,256,768]{2,1,0:T(8,128)(2,1)}) custom-call(bf16[64,96,128]{2,1,0:T(8,128)(2,1)} %bitcast.83, bf16[64,96,128]{2,1,0:T(8,128)(2,1)} %bitcast.84, bf16[256,768]{1,0:T(8,128)(2,1)} %bitcast.94, ...), custom_call_target="tpu_custom_call" | custom-call | tf_op jit(solution)/shard_map/pallas_call | solution.py:95
  177.3 0.0 copy-start.4
  177.3 0.0 copy-start.7
  177.3 3.9 %convolution_bitcast_fusion = f32[384,768]{1,0:T(8,128)S(1)} fusion(bf16[16,128,768]{2,1,0:T(8,128)(2,1)} %bitcast.101, bf16[384,16,128]{2,1,0:T(8,128)(2,1)} %bitcast.104), kind=kOutput, calls=%fused_computation.8 | convolution fusion | flops 1207959552 | bytes 5898240 | tf_op jit(solution)/shard_map/dot_general | solution.py:155
  181.2 0.0 copy-done.4
  181.3 0.0 copy-done.7
  181.3 2.4 convolution_bitcast_fusion.1
  183.7 2.3 copy.57
  186.0 0.0 copy-start.6
  186.0 0.0 copy-start.8
  186.0 4.1 %multiply_reduce_fusion = (bf16[384]{0:T(512)(128)(2,1)S(1)}, f32[384,768]{1,0:T(8,128)S(1)}) fusion(f32[384,768]{1,0:T(8,128)} %convolution_bitcast_fusion.1, f32[384,768]{1,0:T(8,128)S(1)} %convolution_bitcast_fusion, bf16[384,16,128]{0,2,1:T(8,128)(2,1)S(1)} %copy.57, bf16[16,128,768]{2,1,0:T(8,128)(2,1)} %bitcast.103), kind=kOutput, calls=%fused_computation.13 | convolution fusion | flops 1210023552 | bytes 8258304 | tf_op jit(solution)/shard_map/dot_general | solution.py:159
  190.1 0.0 copy-done.6
  190.1 0.0 copy-done.8
  190.1 0.0 copy-start.5
  190.1 1.6 fusion.6
  191.7 0.3 copy-done.5
  192.0 1.5 add_convert_fusion
  193.5 2.2 copy.55
  195.6 0.2 convert_element_type.72
  195.8 0.7 scatter.13.refs_1_
  196.5 4.8 %convolution_convert_fusion = bf16[16,128,768]{2,1,0:T(8,128)(2,1)} fusion(bf16[384,16,128]{0,2,1:T(8,128)(2,1)S(1)} %copy.57, f32[384,768]{1,0:T(8,128)} %convolution_bitcast_fusion.1, f32[384,768]{1,0:T(8,128)S(1)} %convolution_bitcast_fusion), kind=kOutput, calls=%fused_computation.6 | convolution fusion | flops 1211301888 | bytes 7077888 | tf_op jit(solution)/shard_map/dot_general | solution.py:169
  201.3 92.2 %shard_map.95 = (bf16[64,96,128]{2,1,0:T(8,128)(2,1)}, bf16[64,8,128]{2,1,0:T(8,128)(2,1)}, bf16[8,256,768]{2,1,0:T(8,128)(2,1)}) custom-call(bf16[64,96,128]{2,1,0:T(8,128)(2,1)} %bitcast.86, bf16[64,8,128]{2,1,0:T(8,128)(2,1)} %scatter.13.refs_1_, bf16[8,256,768]{2,1,0:T(8,128)(2,1)} %bitcast.88), custom_call_target="tpu_custom_call" | custom-call | tf_op jit(solution)/shard_map/pallas_call | solution.py:95
  293.6 2.1 copy.58
  295.7 0.6 fusion.14
  296.4 0.1 convert_element_type.67
  296.4 1.0 copy.60
  297.5 1.0 slice_reduce_fusion.1
  298.5 0.1 reshape_squeeze.3
  298.6 1.9 gather_fusion.1
  300.6 0.1 reshape.165
  300.8 0.6 copy.61
  301.4 2.4 convert_reduce_fusion
  303.8 1.1 copy.62
  (10 shorter events, 0.1 us)
Async XLA Ops:
  0.6 4.5 %copy-start = (bf16[128,2048]{1,0:T(8,128)(2,1)S(1)}, bf16[128,2048]{1,0:T(8,128)(2,1)}, u32[]{:S(2)}) copy-start(bf16[128,2048]{1,0:T(8,128)(2,1)} %param.9) | copy-start | bytes 1572868
  5.8 2.2 copy-start.3
  7.9 3.1 %copy-start.1 = (bf16[128,2048]{1,0:T(8,128)(2,1)S(1)}, bf16[128,2048]{1,0:T(8,128)(2,1)}, u32[]{:S(2)}) copy-start(bf16[128,2048]{1,0:T(8,128)(2,1)} %param.12) | copy-start | bytes 1572868
  11.6 2.2 copy-start.2
  177.3 3.9 %copy-start.4 = (bf16[8,256,768]{2,1,0:T(8,128)(2,1)S(1)}, bf16[8,256,768]{2,1,0:T(8,128)(2,1)}, u32[]{:S(2)}) copy-start(bf16[8,256,768]{2,1,0:T(8,128)(2,1)} %get-tuple-element.26) | copy-start | bytes 9437188
  177.3 3.9 %copy-start.7 = (bf16[64,96,128]{2,1,0:T(8,128)(2,1)S(1)}, bf16[64,96,128]{2,1,0:T(8,128)(2,1)}, u32[]{:S(2)}) copy-start(bf16[64,96,128]{2,1,0:T(8,128)(2,1)} %get-tuple-element.25) | copy-start | bytes 4718596
  186.0 4.1 %copy-start.6 = (bf16[8,256,768]{2,1,0:T(8,128)(2,1)S(1)}, bf16[8,256,768]{2,1,0:T(8,128)(2,1)}, u32[]{:S(2)}) copy-start(bf16[8,256,768]{2,1,0:T(8,128)(2,1)} %get-tuple-element.27) | copy-start | bytes 9437188
  186.0 4.1 %copy-start.8 = (f32[384,768]{1,0:T(8,128)S(1)}, f32[384,768]{1,0:T(8,128)}, u32[]{:S(2)}) copy-start(f32[384,768]{1,0:T(8,128)} %convolution_bitcast_fusion.1) | copy-start | bytes 3538948
  190.1 1.9 copy-start.5

commit v5 on v4

--- a/solution.py
+++ b/solution.py
@@ -134,8 +134,11 @@
     g_rows = lax.dot_general(
         pick, grad_out.reshape(count, lanes, 128), select, preferred_element_type=jnp.float32
     )
-    padded_gates = jnp.concatenate([gates.reshape(routed), jnp.zeros((1,), jnp.float32)], axis=0)
-    s_send = (padded_gates[owner][:, None, None] * g_rows).astype(jnp.bfloat16)
+    route_ids = jnp.arange(routed, dtype=jnp.int32)
+    slot_gate = jnp.sum(
+        jnp.where(owner[:, None] == route_ids[None, :], gates.reshape(1, routed), 0.0), axis=1
+    )
+    s_send = (slot_gate[:, None, None] * g_rows).astype(jnp.bfloat16)
     dense = (experts, cap * lanes, 128)
     share = w_gate.shape[1]
     hid = w_gate.shape[2]
@@ -185,8 +188,12 @@
         preferred_element_type=jnp.float32,
     )
     grad_tokens = summed.astype(jnp.bfloat16).reshape(count, width)
-    back_scores = score_back[:, 0, :cap].reshape(slots)
-    grad_gates = back_scores[position].astype(jnp.float32).reshape(count, top) / gates
+    back_scores = score_back[:, 0, :cap].reshape(1, slots).astype(jnp.float32)
+    slot_ids = jnp.arange(slots, dtype=jnp.int32)
+    route_score = jnp.sum(
+        jnp.where(position[:, None] == slot_ids[None, :], back_scores, 0.0), axis=1
+    )
+    grad_gates = route_score.reshape(count, top) / gates
     return (grad_tokens, grad_gates, grad_down)
 
 

time: 306 us -> 299 us (0.977)
  matrix products: 20.2 us -> 15.4 us
  local copies, waits for them, and re-layouts: 25 us -> 21.1 us
    gather x2 -> x0, local copies, waits for them, and re-layouts: 4.73 us -> none  [the longest x1 2.8 us: per_device(): s_send = (padded_gates[owner][:, None, None] * g_rows).astype(jnp.bfloat16)]
    unnamed x24 -> x18, local copies, waits for them, and re-layouts: 4.95 us -> 7 us
where the time goes in v5:
time: 299 us; the launch traced here: 298 us
  Pallas kernels  255 us (85%)
  local copies, waits for them, and re-layouts  21.1 us (7%)
  matrix products  15.4 us (5%)
  other arithmetic  5.43 us (2%)
    pallas_call x2, Pallas kernels, exchange(): pl.pallas_call(functools.partial(xfer_kernel, plan, sizes), out_shape=[ja...  255 us
    unnamed x18, local copies, waits for them, and re-layouts  7 us

profile of v5, /device:TPU:1, one launch (start us, length us, event | category | flops | bytes accessed | tf_op | source)
XLA Modules:
  0.0 298.0 jit_solution(13740972147424584386)
XLA Ops:
  0.6 0.0 copy-start
  0.6 0.7 broadcast_multiply_fusion
  1.4 0.1 copy.63
  1.5 0.1 mul.60
  1.6 0.8 copy.69
  2.4 0.1 broadcast_in_dim.43
  2.6 0.8 copy.64
  3.4 0.1 eq.64
  3.5 0.1 eq.68
  3.7 0.6 reduce-window.6
  4.3 0.2 slice_reduce_fusion
  4.5 0.1 fusion.23
  4.6 1.4 scatter_custom_fusion
  6.0 0.2 select_reduce_fusion.1
  6.3 1.9 copy.72
  8.2 0.0 copy-done
  8.2 0.6 multiply_convert_fusion
  8.8 0.0 copy-start.1
  8.8 2.1 copy.71
  11.0 0.0 copy-done.1
  11.0 0.6 convolution_convert_fusion.1
  11.6 2.2 copy.68
  13.8 162.7 %shard_map.94 = (bf16[64,96,128]{2,1,0:T(8,128)(2,1)}, bf16[64,96,128]{2,1,0:T(8,128)(2,1)}, bf16[8,256,768]{2,1,0:T(8,128)(2,1)}, bf16[8,256,768]{2,1,0:T(8,128)(2,1)}, bf16[8,256,768]{2,1,0:T(8,128)(2,1)}) custom-call(bf16[64,96,128]{2,1,0:T(8,128)(2,1)} %bitcast.85, bf16[64,96,128]{2,1,0:T(8,128)(2,1)} %bitcast.84, bf16[256,768]{1,0:T(8,128)(2,1)} %bitcast.95, ...), custom_call_target="tpu_custom_call" | custom-call | tf_op jit(solution)/shard_map/pallas_call | solution.py:95
  176.5 2.1 copy.78
  178.6 0.0 copy-start.2
  178.6 0.0 copy-start.5
  178.7 3.9 %convolution_bitcast_fusion = f32[384,768]{1,0:T(8,128)S(1)} fusion(bf16[16,128,768]{2,1,0:T(8,128)(2,1)} %bitcast.101, bf16[384,16,128]{2,1,0:T(8,128)(2,1)} %bitcast.104), kind=kOutput, calls=%fused_computation.6 | convolution fusion | flops 1207959552 | bytes 5898240 | tf_op jit(solution)/shard_map/dot_general | solution.py:158
  182.6 0.0 copy-done.2
  182.6 0.0 copy-done.5
  182.6 0.0 copy-start.4
  182.6 1.4 convolution_bitcast_fusion.1
  184.0 0.5 copy-done.4
  184.5 0.0 copy-start.3
  184.5 1.7 multiply_reduce_fusion
  186.2 0.2 copy-done.3
  186.4 1.6 fusion.6
  187.9 1.4 add_convert_fusion
  189.4 3.6 %convolution_convert_fusion = bf16[16,128,768]{2,1,0:T(8,128)(2,1)} fusion(bf16[384,16,128]{0,2,1:T(8,128)(2,1)S(1)} %copy.78, f32[384,768]{1,0:T(8,128)S(1)} %convolution_bitcast_fusion.1, f32[384,768]{1,0:T(8,128)S(1)} %convolution_bitcast_fusion), kind=kOutput, calls=%fused_computation.4 | convolution fusion | flops 1211301888 | bytes 7077888 | tf_op jit(solution)/shard_map/dot_general | solution.py:172
  192.9 2.2 copy.76
  195.1 0.2 convert_element_type.76
  195.2 0.7 scatter.13.refs_1_
  195.9 92.5 %shard_map.95 = (bf16[64,96,128]{2,1,0:T(8,128)(2,1)}, bf16[64,8,128]{2,1,0:T(8,128)(2,1)}, bf16[8,256,768]{2,1,0:T(8,128)(2,1)}) custom-call(bf16[64,96,128]{2,1,0:T(8,128)(2,1)} %bitcast.87, bf16[64,8,128]{2,1,0:T(8,128)(2,1)} %scatter.13.refs_1_, bf16[8,256,768]{2,1,0:T(8,128)(2,1)} %bitcast.89), custom_call_target="tpu_custom_call" | custom-call | tf_op jit(solution)/shard_map/pallas_call | solution.py:95
  288.4 2.1 copy.79
  290.5 0.7 fusion.14
  291.2 0.1 convert_element_type.71
  291.3 1.0 copy.81
  292.3 1.0 convert_reduce_fusion.1
  293.3 0.1 reshape.178
  293.4 0.2 select_reduce_fusion
  293.6 0.1 reshape.177
  293.8 0.6 copy.82
  294.4 2.4 convert_reduce_fusion
  296.8 1.1 copy.83
  (8 shorter events, 0.1 us)
Async XLA Ops:
  0.6 7.6 %copy-start = (bf16[128,2048]{1,0:T(8,128)(2,1)S(1)}, bf16[128,2048]{1,0:T(8,128)(2,1)}, u32[]{:S(2)}) copy-start(bf16[128,2048]{1,0:T(8,128)(2,1)} %param.12) | copy-start | bytes 1572868
  8.8 2.2 copy-start.1
  178.6 3.9 %copy-start.2 = (bf16[8,256,768]{2,1,0:T(8,128)(2,1)S(1)}, bf16[8,256,768]{2,1,0:T(8,128)(2,1)}, u32[]{:S(2)}) copy-start(bf16[8,256,768]{2,1,0:T(8,128)(2,1)} %get-tuple-element.26) | copy-start | bytes 9437188
  178.6 3.9 %copy-start.5 = (bf16[64,96,128]{2,1,0:T(8,128)(2,1)S(1)}, bf16[64,96,128]{2,1,0:T(8,128)(2,1)}, u32[]{:S(2)}) copy-start(bf16[64,96,128]{2,1,0:T(8,128)(2,1)} %get-tuple-element.25) | copy-start | bytes 4718596
  182.6 1.9 copy-start.4
  184.5 1.9 copy-start.3

commit v6 on v4

--- a/solution.py
+++ b/solution.py
@@ -117,16 +117,13 @@
     slots = experts * cap
     routed = count * top
     flat = routes.reshape(routed)
-    labels = jnp.arange(experts, dtype=jnp.int32)
-    onehot = (flat[:, None] == labels[None, :]).astype(jnp.int32)
-    rank = jnp.sum((jnp.cumsum(onehot, axis=0) - onehot) * onehot, axis=1)
+    route_ids = jnp.arange(routed, dtype=jnp.int32)
+    same = (flat[:, None] == flat[None, :]) & (route_ids[None, :] < route_ids[:, None])
+    rank = jnp.sum(same.astype(jnp.int32), axis=1)
     position = flat * cap + rank
-    owner = (
-        jnp.full((slots,), routed, jnp.int32).at[position].set(jnp.arange(routed, dtype=jnp.int32))
-    )
-    source = owner // top
+    hit = position[None, :] == jnp.arange(slots, dtype=jnp.int32)[:, None]
     lanes = width // 128
-    pick = (source[:, None] == jnp.arange(count, dtype=jnp.int32)[None, :]).astype(jnp.bfloat16)
+    pick = jnp.any(hit.reshape(slots, count, top), axis=2).astype(jnp.bfloat16)
     select = (((1,), (0,)), ((), ()))
     x_send = lax.dot_general(
         pick, tokens.reshape(count, lanes, 128), select, preferred_element_type=jnp.float32
@@ -134,8 +131,8 @@
     g_rows = lax.dot_general(
         pick, grad_out.reshape(count, lanes, 128), select, preferred_element_type=jnp.float32
     )
-    padded_gates = jnp.concatenate([gates.reshape(routed), jnp.zeros((1,), jnp.float32)], axis=0)
-    s_send = (padded_gates[owner][:, None, None] * g_rows).astype(jnp.bfloat16)
+    slot_gate = jnp.sum(jnp.where(hit, gates.reshape(1, routed), 0.0), axis=1)
+    s_send = (slot_gate[:, None, None] * g_rows).astype(jnp.bfloat16)
     dense = (experts, cap * lanes, 128)
     share = w_gate.shape[1]
     hid = w_gate.shape[2]
@@ -185,8 +182,9 @@
         preferred_element_type=jnp.float32,
     )
     grad_tokens = summed.astype(jnp.bfloat16).reshape(count, width)
-    back_scores = score_back[:, 0, :cap].reshape(slots)
-    grad_gates = back_scores[position].astype(jnp.float32).reshape(count, top) / gates
+    back_scores = score_back[:, 0, :cap].reshape(slots, 1).astype(jnp.float32)
+    route_score = jnp.sum(jnp.where(hit, back_scores, 0.0), axis=0)
+    grad_gates = route_score.reshape(count, top) / gates
     return (grad_tokens, grad_gates, grad_down)
 
 

time: 306 us -> 296 us (0.967)
  local copies, waits for them, and re-layouts: 25 us -> 19.4 us
  matrix products: 20.2 us -> 15.2 us
    gather x2 -> x0, local copies, waits for them, and re-layouts: 4.73 us -> none  [the longest x1 2.8 us: per_device(): s_send = (padded_gates[owner][:, None, None] * g_rows).astype(jnp.bfloat16)]
    unnamed x24 -> x18, local copies, waits for them, and re-layouts: 4.95 us -> 7.04 us
where the time goes in v6:
time: 296 us; the launch traced here: 295 us
  Pallas kernels  255 us (86%)
  local copies, waits for them, and re-layouts  19.4 us (7%)
  matrix products  15.2 us (5%)
  other arithmetic  4.72 us (2%)
    pallas_call x2, Pallas kernels, exchange(): pl.pallas_call(functools.partial(xfer_kernel, plan, sizes), out_shape=[ja...  255 us
    unnamed x18, local copies, waits for them, and re-layouts  7.04 us

profile of v6, /device:TPU:1, one launch (start us, length us, event | category | flops | bytes accessed | tf_op | source)
XLA Modules:
  0.0 295.3 jit_solution(9156059705671261238)
XLA Ops:
  0.6 0.0 copy-start
  0.6 0.8 copy.87
  1.5 0.1 broadcast_in_dim.33
  1.6 0.8 copy.83
  2.4 0.1 eq.35
  2.6 0.2 convert_reduce_fusion.1
  2.8 0.2 select_reduce_fusion.1
  2.9 0.1 reduce_sum.48
  3.1 0.1 copy.84
  3.1 0.7 multiply_add_fusion.1
  3.9 1.9 copy.90
  5.8 0.0 copy-done
  5.8 0.6 multiply_convert_fusion
  6.4 0.0 copy-start.1
  6.4 2.1 copy.89
  8.5 0.0 copy-done.1
  8.5 0.6 convolution_convert_fusion.1
  9.1 2.2 copy.86
  11.3 162.7 %shard_map.94 = (bf16[64,96,128]{2,1,0:T(8,128)(2,1)}, bf16[64,96,128]{2,1,0:T(8,128)(2,1)}, bf16[8,256,768]{2,1,0:T(8,128)(2,1)}, bf16[8,256,768]{2,1,0:T(8,128)(2,1)}, bf16[8,256,768]{2,1,0:T(8,128)(2,1)}) custom-call(bf16[64,96,128]{2,1,0:T(8,128)(2,1)} %bitcast.65, bf16[64,96,128]{2,1,0:T(8,128)(2,1)} %bitcast.64, bf16[256,768]{1,0:T(8,128)(2,1)} %bitcast.75, ...), custom_call_target="tpu_custom_call" | custom-call | tf_op jit(solution)/shard_map/pallas_call | solution.py:95
  174.0 2.1 copy.96
  176.1 0.0 copy-start.2
  176.1 0.0 copy-start.5
  176.1 3.9 %convolution_bitcast_fusion = f32[384,768]{1,0:T(8,128)S(1)} fusion(bf16[16,128,768]{2,1,0:T(8,128)(2,1)} %bitcast.79, bf16[384,16,128]{2,1,0:T(8,128)(2,1)} %bitcast.82), kind=kOutput, calls=%fused_computation.5 | convolution fusion | flops 1207959552 | bytes 5898240 | tf_op jit(solution)/shard_map/dot_general | solution.py:152
  180.0 0.0 copy-done.2
  180.0 0.0 copy-done.5
  180.1 0.0 copy-start.4
  180.1 1.4 convolution_bitcast_fusion.1
  181.5 0.5 copy-done.4
  181.9 0.0 copy-start.3
  182.0 1.7 multiply_reduce_fusion
  183.7 0.2 copy-done.3
  183.8 1.6 fusion.6
  185.4 1.4 add_convert_fusion
  186.8 3.6 %convolution_convert_fusion = bf16[16,128,768]{2,1,0:T(8,128)(2,1)} fusion(bf16[384,16,128]{0,2,1:T(8,128)(2,1)S(1)} %copy.96, f32[384,768]{1,0:T(8,128)S(1)} %convolution_bitcast_fusion.1, f32[384,768]{1,0:T(8,128)S(1)} %convolution_bitcast_fusion), kind=kOutput, calls=%fused_computation.3 | convolution fusion | flops 1211301888 | bytes 7077888 | tf_op jit(solution)/shard_map/dot_general | solution.py:166
  190.4 2.2 copy.94
  192.6 0.2 convert_element_type.71
  192.7 0.7 scatter.4.refs_1_
  193.4 92.4 %shard_map.95 = (bf16[64,96,128]{2,1,0:T(8,128)(2,1)}, bf16[64,8,128]{2,1,0:T(8,128)(2,1)}, bf16[8,256,768]{2,1,0:T(8,128)(2,1)}) custom-call(bf16[64,96,128]{2,1,0:T(8,128)(2,1)} %bitcast.66, bf16[64,8,128]{2,1,0:T(8,128)(2,1)} %scatter.4.refs_1_, bf16[8,256,768]{2,1,0:T(8,128)(2,1)} %bitcast.69), custom_call_target="tpu_custom_call" | custom-call | tf_op jit(solution)/shard_map/pallas_call | solution.py:95
  285.8 2.1 copy.97
  287.9 0.6 fusion.21
  288.5 0.1 convert_element_type.66
  288.6 1.0 copy.99
  289.7 1.0 convert_reduce_fusion.2
  290.6 0.1 reshape.145
  290.8 0.1 select_reduce_fusion
  290.9 0.1 reshape.144
  291.1 0.6 copy.100
  291.7 2.4 convert_reduce_fusion
  294.1 1.1 copy.101
  (3 shorter events, 0.1 us)
Async XLA Ops:
  0.6 5.2 %copy-start = (bf16[128,2048]{1,0:T(8,128)(2,1)S(1)}, bf16[128,2048]{1,0:T(8,128)(2,1)}, u32[]{:S(2)}) copy-start(bf16[128,2048]{1,0:T(8,128)(2,1)} %param.12) | copy-start | bytes 1572868
  6.4 2.2 copy-start.1
  176.1 3.9 %copy-start.2 = (bf16[8,256,768]{2,1,0:T(8,128)(2,1)S(1)}, bf16[8,256,768]{2,1,0:T(8,128)(2,1)}, u32[]{:S(2)}) copy-start(bf16[8,256,768]{2,1,0:T(8,128)(2,1)} %get-tuple-element.26) | copy-start | bytes 9437188
  176.1 3.9 %copy-start.5 = (bf16[64,96,128]{2,1,0:T(8,128)(2,1)S(1)}, bf16[64,96,128]{2,1,0:T(8,128)(2,1)}, u32[]{:S(2)}) copy-start(bf16[64,96,128]{2,1,0:T(8,128)(2,1)} %get-tuple-element.25) | copy-start | bytes 4718596
  180.1 1.9 copy-start.4
  181.9 1.9 copy-start.3

commit v7 on v6

--- a/solution.py
+++ b/solution.py
@@ -116,14 +116,14 @@
     cap = 3 * count * top // (2 * experts)
     slots = experts * cap
     routed = count * top
-    flat = routes.reshape(routed)
+    flat = routes.T.reshape(routed)
     route_ids = jnp.arange(routed, dtype=jnp.int32)
     same = (flat[:, None] == flat[None, :]) & (route_ids[None, :] < route_ids[:, None])
     rank = jnp.sum(same.astype(jnp.int32), axis=1)
     position = flat * cap + rank
     hit = position[None, :] == jnp.arange(slots, dtype=jnp.int32)[:, None]
     lanes = width // 128
-    pick = jnp.any(hit.reshape(slots, count, top), axis=2).astype(jnp.bfloat16)
+    pick = jnp.any(hit.reshape(slots, top, count), axis=1).astype(jnp.bfloat16)
     select = (((1,), (0,)), ((), ()))
     x_send = lax.dot_general(
         pick, tokens.reshape(count, lanes, 128), select, preferred_element_type=jnp.float32
@@ -131,7 +131,7 @@
     g_rows = lax.dot_general(
         pick, grad_out.reshape(count, lanes, 128), select, preferred_element_type=jnp.float32
     )
-    slot_gate = jnp.sum(jnp.where(hit, gates.reshape(1, routed), 0.0), axis=1)
+    slot_gate = jnp.sum(jnp.where(hit, gates.T.reshape(1, routed), 0.0), axis=1)
     s_send = (slot_gate[:, None, None] * g_rows).astype(jnp.bfloat16)
     dense = (experts, cap * lanes, 128)
     share = w_gate.shape[1]
@@ -184,7 +184,7 @@
     grad_tokens = summed.astype(jnp.bfloat16).reshape(count, width)
     back_scores = score_back[:, 0, :cap].reshape(slots, 1).astype(jnp.float32)
     route_score = jnp.sum(jnp.where(hit, back_scores, 0.0), axis=0)
-    grad_gates = route_score.reshape(count, top) / gates
+    grad_gates = route_score.reshape(top, count).T / gates
     return (grad_tokens, grad_gates, grad_down)
 
 

time: 296 us -> 296 us (level)
    unnamed x18 -> x17, local copies, waits for them, and re-layouts: 7.04 us -> 4.86 us
where the time goes in v7:
time: 296 us; the launch traced here: 295 us
  Pallas kernels  255 us (86%)
  local copies, waits for them, and re-layouts  16.6 us (6%)
  matrix products  15.2 us (5%)
  other arithmetic  7.36 us (2%)
    pallas_call x2, Pallas kernels, exchange(): pl.pallas_call(functools.partial(xfer_kernel, plan, sizes), out_shape=[ja...  255 us

profile of v7, /device:TPU:1, one launch (start us, length us, event | category | flops | bytes accessed | tf_op | source)
XLA Modules:
  0.0 295.1 jit_solution(7577537713164983447)
XLA Ops:
  0.6 0.0 copy-start
  0.6 0.9 convert_reduce_fusion.1
  1.6 0.7 multiply_add_fusion
  2.3 0.7 bitcast_add_fusion
  2.9 0.8 select_reduce_fusion.1
  3.8 1.9 copy.53
  5.7 0.0 copy-done
  5.7 0.6 multiply_convert_fusion
  6.3 0.0 copy-start.1
  6.3 2.1 copy.52
  8.5 0.0 copy-done.1
  8.5 0.6 convolution_convert_fusion.1
  9.0 2.2 copy.50
  11.2 162.7 %shard_map.94 = (bf16[64,96,128]{2,1,0:T(8,128)(2,1)}, bf16[64,96,128]{2,1,0:T(8,128)(2,1)}, bf16[8,256,768]{2,1,0:T(8,128)(2,1)}, bf16[8,256,768]{2,1,0:T(8,128)(2,1)}, bf16[8,256,768]{2,1,0:T(8,128)(2,1)}) custom-call(bf16[64,96,128]{2,1,0:T(8,128)(2,1)} %bitcast.81, bf16[64,96,128]{2,1,0:T(8,128)(2,1)} %bitcast.80, bf16[256,768]{1,0:T(8,128)(2,1)} %bitcast.91, ...), custom_call_target="tpu_custom_call" | custom-call | tf_op jit(solution)/shard_map/pallas_call | solution.py:95
  174.0 2.1 copy.59
  176.1 0.0 copy-start.3
  176.1 0.0 copy-start.6
  176.1 3.9 %convolution_bitcast_fusion = f32[384,768]{1,0:T(8,128)S(1)} fusion(bf16[16,128,768]{2,1,0:T(8,128)(2,1)} %bitcast.97, bf16[384,16,128]{2,1,0:T(8,128)(2,1)} %bitcast.100), kind=kOutput, calls=%fused_computation.5 | convolution fusion | flops 1207959552 | bytes 5898240 | tf_op jit(solution)/shard_map/dot_general | solution.py:152
  180.0 0.0 copy-done.3
  180.0 0.0 copy-done.6
  180.0 0.0 copy-start.5
  180.0 1.4 convolution_bitcast_fusion.1
  181.4 0.5 copy-done.5
  181.9 0.0 copy-start.4
  181.9 1.6 multiply_reduce_fusion
  183.6 0.2 copy-done.4
  183.8 1.6 fusion.6
  185.4 1.4 add_convert_fusion
  186.8 3.6 %convolution_convert_fusion = bf16[16,128,768]{2,1,0:T(8,128)(2,1)} fusion(bf16[384,16,128]{0,2,1:T(8,128)(2,1)S(1)} %copy.59, f32[384,768]{1,0:T(8,128)S(1)} %convolution_bitcast_fusion.1, f32[384,768]{1,0:T(8,128)S(1)} %convolution_bitcast_fusion), kind=kOutput, calls=%fused_computation.3 | convolution fusion | flops 1211301888 | bytes 7077888 | tf_op jit(solution)/shard_map/dot_general | solution.py:166
  190.4 2.2 copy.57
  192.5 0.2 convert_element_type.71
  192.7 0.7 scatter.4.refs_1_
  193.4 92.4 %shard_map.95 = (bf16[64,96,128]{2,1,0:T(8,128)(2,1)}, bf16[64,8,128]{2,1,0:T(8,128)(2,1)}, bf16[8,256,768]{2,1,0:T(8,128)(2,1)}) custom-call(bf16[64,96,128]{2,1,0:T(8,128)(2,1)} %bitcast.82, bf16[64,8,128]{2,1,0:T(8,128)(2,1)} %scatter.4.refs_1_, bf16[8,256,768]{2,1,0:T(8,128)(2,1)} %bitcast.85), custom_call_target="tpu_custom_call" | custom-call | tf_op jit(solution)/shard_map/pallas_call | solution.py:95
  285.8 2.1 copy.60
  287.9 0.6 fusion.21
  288.5 0.0 copy-start.2
  288.5 0.1 convert_element_type.66
  288.6 1.0 copy.61
  289.6 1.0 convert_reduce_fusion.2
  290.6 0.1 reshape.145
  290.8 0.1 select_reduce_fusion
  290.9 0.0 copy-done.2
  290.9 0.6 bitcast_divide_fusion
  291.5 2.4 convert_reduce_fusion
  293.9 1.1 copy.62
  (1 shorter events, 0.0 us)
Async XLA Ops:
  0.6 5.1 %copy-start = (bf16[128,2048]{1,0:T(8,128)(2,1)S(1)}, bf16[128,2048]{1,0:T(8,128)(2,1)}, u32[]{:S(2)}) copy-start(bf16[128,2048]{1,0:T(8,128)(2,1)} %param.12) | copy-start | bytes 1572868
  6.3 2.2 copy-start.1
  176.1 3.9 %copy-start.3 = (bf16[8,256,768]{2,1,0:T(8,128)(2,1)S(1)}, bf16[8,256,768]{2,1,0:T(8,128)(2,1)}, u32[]{:S(2)}) copy-start(bf16[8,256,768]{2,1,0:T(8,128)(2,1)} %get-tuple-element.26) | copy-start | bytes 9437188
  176.1 3.9 %copy-start.6 = (bf16[64,96,128]{2,1,0:T(8,128)(2,1)S(1)}, bf16[64,96,128]{2,1,0:T(8,128)(2,1)}, u32[]{:S(2)}) copy-start(bf16[64,96,128]{2,1,0:T(8,128)(2,1)} %get-tuple-element.25) | copy-start | bytes 4718596
  180.0 1.9 copy-start.5
  181.9 1.9 copy-start.4
  288.5 2.4 copy-start.2

commit v8 on v7

--- a/solution.py
+++ b/solution.py
@@ -134,12 +134,16 @@
     slot_gate = jnp.sum(jnp.where(hit, gates.T.reshape(1, routed), 0.0), axis=1)
     s_send = (slot_gate[:, None, None] * g_rows).astype(jnp.bfloat16)
     dense = (experts, cap * lanes, 128)
+    eye = jnp.eye(w_down.shape[2], dtype=w_down.dtype)
+    down_t = lax.dot_general(
+        eye, w_down[0], (((1,), (1,)), ((), ())), preferred_element_type=jnp.float32
+    ).astype(w_down.dtype)
     share = w_gate.shape[1]
     hid = w_gate.shape[2]
     x_in, s_in, gate_all, up_all, down_all = exchange(
         (("a2a", "expert"), ("a2a", "expert"), ("gather", "dp"), ("gather", "dp"), ("gather", "dp")),
         sizes,
-        (x_send.reshape(dense), s_send.reshape(dense), w_gate[0], w_up[0], w_down[0].T),
+        (x_send.reshape(dense), s_send.reshape(dense), w_gate[0], w_up[0], down_t),
         (dense, dense, (groups, share, hid), (groups, share, hid), (groups, share, hid)),
         0,
     )

time: 296 us -> 296 us (level)
  no operation moved by 1% of the time
where the time goes in v8:
time: 296 us; the launch traced here: 295 us
  Pallas kernels  255 us (86%)
  matrix products  17.2 us (6%)
  local copies, waits for them, and re-layouts  14.6 us (5%)
  other arithmetic  7.36 us (2%)
    pallas_call x2, Pallas kernels, exchange(): pl.pallas_call(functools.partial(xfer_kernel, plan, sizes), out_shape=[ja...  255 us

profile of v8, /device:TPU:1, one launch (start us, length us, event | category | flops | bytes accessed | tf_op | source)
XLA Modules:
  0.0 295.2 jit_solution(6344243454558555935)
XLA Ops:
  0.6 0.0 copy-start
  0.6 0.9 convert_reduce_fusion.1
  1.6 0.7 multiply_add_fusion
  2.3 0.7 bitcast_add_fusion
  2.9 0.8 select_reduce_fusion.1
  3.8 2.1 convolution_convert_fusion.2.refs_4_
  5.9 0.0 copy-done
  5.9 0.6 multiply_convert_fusion
  6.5 0.0 copy-start.1
  6.5 2.1 copy.49
  8.6 0.0 copy-done.1
  8.6 0.6 convolution_convert_fusion.1
  9.2 2.2 copy.47
  11.4 162.7 %shard_map.94 = (bf16[64,96,128]{2,1,0:T(8,128)(2,1)}, bf16[64,96,128]{2,1,0:T(8,128)(2,1)}, bf16[8,256,768]{2,1,0:T(8,128)(2,1)}, bf16[8,256,768]{2,1,0:T(8,128)(2,1)}, bf16[8,256,768]{2,1,0:T(8,128)(2,1)}) custom-call(bf16[64,96,128]{2,1,0:T(8,128)(2,1)} %bitcast.81, bf16[64,96,128]{2,1,0:T(8,128)(2,1)} %bitcast.80, bf16[256,768]{1,0:T(8,128)(2,1)} %bitcast.90, ...), custom_call_target="tpu_custom_call" | custom-call | tf_op jit(solution)/shard_map/pallas_call | solution.py:95
  174.1 2.1 copy.55
  176.2 0.0 copy-start.3
  176.2 0.0 copy-start.6
  176.2 3.9 %convolution_bitcast_fusion = f32[384,768]{1,0:T(8,128)S(1)} fusion(bf16[16,128,768]{2,1,0:T(8,128)(2,1)} %bitcast.96, bf16[384,16,128]{2,1,0:T(8,128)(2,1)} %bitcast.99), kind=kOutput, calls=%fused_computation.5 | convolution fusion | flops 1207959552 | bytes 5898240 | tf_op jit(solution)/shard_map/dot_general | solution.py:156
  180.1 0.0 copy-done.3
  180.1 0.0 copy-done.6
  180.2 0.0 copy-start.5
  180.2 1.4 convolution_bitcast_fusion.1
  181.6 0.5 copy-done.5
  182.0 0.0 copy-start.4
  182.0 1.7 multiply_reduce_fusion
  183.7 0.2 copy-done.4
  183.9 1.6 fusion.6
  185.5 1.4 add_convert_fusion
  186.9 3.6 %convolution_convert_fusion = bf16[16,128,768]{2,1,0:T(8,128)(2,1)} fusion(bf16[384,16,128]{0,2,1:T(8,128)(2,1)S(1)} %copy.55, f32[384,768]{1,0:T(8,128)S(1)} %convolution_bitcast_fusion.1, f32[384,768]{1,0:T(8,128)S(1)} %convolution_bitcast_fusion), kind=kOutput, calls=%fused_computation.3 | convolution fusion | flops 1211301888 | bytes 7077888 | tf_op jit(solution)/shard_map/dot_general | solution.py:170
  190.5 2.2 copy.53
  192.7 0.2 convert_element_type.76
  192.8 0.7 scatter.4.refs_1_
  193.5 92.5 %shard_map.95 = (bf16[64,96,128]{2,1,0:T(8,128)(2,1)}, bf16[64,8,128]{2,1,0:T(8,128)(2,1)}, bf16[8,256,768]{2,1,0:T(8,128)(2,1)}) custom-call(bf16[64,96,128]{2,1,0:T(8,128)(2,1)} %bitcast.82, bf16[64,8,128]{2,1,0:T(8,128)(2,1)} %scatter.4.refs_1_, bf16[8,256,768]{2,1,0:T(8,128)(2,1)} %bitcast.85), custom_call_target="tpu_custom_call" | custom-call | tf_op jit(solution)/shard_map/pallas_call | solution.py:95
  286.0 2.1 copy.56
  288.1 0.6 fusion.22
  288.7 0.0 copy-start.2
  288.7 0.1 convert_element_type.71
  288.8 1.0 copy.57
  289.8 1.0 convert_reduce_fusion.2
  290.8 0.1 reshape.145
  291.0 0.1 select_reduce_fusion
  291.1 0.0 copy-done.2
  291.1 0.6 bitcast_divide_fusion
  291.7 2.4 convert_reduce_fusion
  294.1 1.1 copy.58
  (1 shorter events, 0.0 us)
Async XLA Ops:
  0.6 5.3 %copy-start = (bf16[128,2048]{1,0:T(8,128)(2,1)S(1)}, bf16[128,2048]{1,0:T(8,128)(2,1)}, u32[]{:S(2)}) copy-start(bf16[128,2048]{1,0:T(8,128)(2,1)} %param.12) | copy-start | bytes 1572868
  6.5 2.2 copy-start.1
  176.2 3.9 %copy-start.3 = (bf16[8,256,768]{2,1,0:T(8,128)(2,1)S(1)}, bf16[8,256,768]{2,1,0:T(8,128)(2,1)}, u32[]{:S(2)}) copy-start(bf16[8,256,768]{2,1,0:T(8,128)(2,1)} %get-tuple-element.26) | copy-start | bytes 9437188
  176.2 3.9 %copy-start.6 = (bf16[64,96,128]{2,1,0:T(8,128)(2,1)S(1)}, bf16[64,96,128]{2,1,0:T(8,128)(2,1)}, u32[]{:S(2)}) copy-start(bf16[64,96,128]{2,1,0:T(8,128)(2,1)} %get-tuple-element.25) | copy-start | bytes 4718596
  180.2 1.9 copy-start.5
  182.0 1.9 copy-start.4
  288.7 2.4 copy-start.2

commit v9 on v7

--- a/solution.py
+++ b/solution.py
@@ -176,7 +176,11 @@
         (dense, (experts, 8, 128), (groups, share, hid)),
         1,
     )
-    grad_down = jnp.sum(parts_in.astype(jnp.float32), axis=0).T[None]
+    fold = jnp.tile(jnp.eye(share, dtype=jnp.bfloat16), (groups, 1))
+    grad_down = lax.dot_general(
+        parts_in.reshape(groups * share, hid), fold, (((0,), (0,)), ((), ())),
+        preferred_element_type=jnp.float32,
+    )[None]
     summed = lax.dot_general(
         pick, rg_back.reshape(slots, lanes, 128), (((0,), (0,)), ((), ())),
         preferred_element_type=jnp.float32,

time: 296 us -> 298 us (level)
  matrix products: 15.2 us -> 23.8 us
  other arithmetic: 7.36 us -> 3.63 us
    dot_general x0 -> x1, matrix products: none -> 3.79 us  [per_device(): lax.dot_general(parts_in.reshape(groups * share, hid), fold, (((0,), (0,)...]
where the time goes in v9:
time: 298 us; the launch traced here: 297 us
  Pallas kernels  255 us (86%)
  matrix products  23.8 us (8%)
  local copies, waits for them, and re-layouts  14 us (5%)
  other arithmetic  3.63 us (1%)
    pallas_call x2, Pallas kernels, exchange(): pl.pallas_call(functools.partial(xfer_kernel, plan, sizes), out_shape=[ja...  255 us

profile of v9, /device:TPU:1, one launch (start us, length us, event | category | flops | bytes accessed | tf_op | source)
XLA Modules:
  0.0 297.5 jit_solution(4138758256199567179)
XLA Ops:
  0.6 0.0 copy-start
  0.6 0.9 convert_reduce_fusion
  1.6 0.7 bitcast_add_fusion
  2.3 0.0 copy-done
  2.3 0.6 convolution_convert_fusion.1
  2.9 0.0 copy-start.3
  2.9 0.0 copy-start.4
  2.9 0.0 copy-start.1
  2.9 2.1 copy.38
  5.1 0.0 copy-done.3
  5.1 0.0 copy-done.4
  5.1 0.1 select_reduce_fusion.1
  5.2 0.0 copy-done.1
  5.2 0.6 multiply_convert_fusion
  5.8 0.0 copy-start.2
  5.8 2.2 copy.40
  8.0 0.0 copy-done.2
  8.0 0.9 copy.41
  9.0 162.7 %shard_map.94 = (bf16[64,96,128]{2,1,0:T(8,128)(2,1)}, bf16[64,96,128]{2,1,0:T(8,128)(2,1)}, bf16[8,256,768]{2,1,0:T(8,128)(2,1)}, bf16[8,256,768]{2,1,0:T(8,128)(2,1)}, bf16[8,256,768]{2,1,0:T(8,128)(2,1)}) custom-call(bf16[64,96,128]{2,1,0:T(8,128)(2,1)} %bitcast.81, bf16[64,96,128]{2,1,0:T(8,128)(2,1)} %bitcast.82, bf16[256,768]{1,0:T(8,128)(2,1)} %bitcast.91, ...), custom_call_target="tpu_custom_call" | custom-call | tf_op jit(solution)/shard_map/pallas_call | solution.py:95
  171.7 0.0 copy-start.5
  171.7 0.0 copy-start.8
  171.7 3.9 %convolution_bitcast_fusion = f32[384,768]{1,0:T(8,128)S(1)} fusion(bf16[16,128,768]{2,1,0:T(8,128)(2,1)} %bitcast.97, bf16[384,16,128]{2,1,0:T(8,128)(2,1)} %bitcast.100), kind=kOutput, calls=%fused_computation.4 | convolution fusion | flops 1207959552 | bytes 5898240 | tf_op jit(solution)/shard_map/dot_general | solution.py:152
  175.6 0.0 copy-done.5
  175.6 0.0 copy-done.8
  175.6 2.4 convolution_bitcast_fusion.1
  178.0 2.1 copy.47
  180.1 0.0 copy-start.7
  180.1 0.0 copy-start.9
  180.2 4.1 %multiply_reduce_fusion = (bf16[384]{0:T(512)(128)(2,1)S(1)}, f32[384,768]{1,0:T(8,128)S(1)}) fusion(f32[384,768]{1,0:T(8,128)} %convolution_bitcast_fusion.1, f32[384,768]{1,0:T(8,128)S(1)} %convolution_bitcast_fusion, bf16[384,16,128]{0,2,1:T(8,128)(2,1)S(1)} %copy.47, bf16[16,128,768]{2,1,0:T(8,128)(2,1)} %bitcast.99), kind=kOutput, calls=%fused_computation.10 | convolution fusion | flops 1210023552 | bytes 8258304 | tf_op jit(solution)/shard_map/dot_general | solution.py:156
  184.2 0.0 copy-done.7
  184.2 0.0 copy-done.9
  184.2 0.0 copy-start.6
  184.3 1.6 fusion.6
  185.9 0.3 copy-done.6
  186.1 1.5 add_convert_fusion
  187.6 2.2 copy.45
  189.8 0.2 convert_element_type.75
  189.9 0.7 scatter.4.refs_1_
  190.6 4.8 %convolution_convert_fusion = bf16[16,128,768]{2,1,0:T(8,128)(2,1)} fusion(bf16[384,16,128]{0,2,1:T(8,128)(2,1)S(1)} %copy.47, f32[384,768]{1,0:T(8,128)} %convolution_bitcast_fusion.1, f32[384,768]{1,0:T(8,128)S(1)} %convolution_bitcast_fusion), kind=kOutput, calls=%fused_computation.2 | convolution fusion | flops 1211301888 | bytes 7077888 | tf_op jit(solution)/shard_map/dot_general | solution.py:166
  195.5 92.5 %shard_map.95 = (bf16[64,96,128]{2,1,0:T(8,128)(2,1)}, bf16[64,8,128]{2,1,0:T(8,128)(2,1)}, bf16[8,256,768]{2,1,0:T(8,128)(2,1)}) custom-call(bf16[64,96,128]{2,1,0:T(8,128)(2,1)} %bitcast.83, bf16[64,8,128]{2,1,0:T(8,128)(2,1)} %scatter.4.refs_1_, bf16[8,256,768]{2,1,0:T(8,128)(2,1)} %bitcast.86), custom_call_target="tpu_custom_call" | custom-call | tf_op jit(solution)/shard_map/pallas_call | solution.py:95
  288.0 2.1 copy.48
  290.1 0.6 fusion.23
  290.7 0.1 convert_element_type.70
  290.8 1.0 copy.50
  291.8 1.0 convert_reduce_fusion.1
  292.8 0.1 reshape.157
  293.0 0.1 select_reduce_fusion
  293.1 0.6 bitcast_divide_fusion
  293.7 3.8 %convolution_bitcast_fusion.3 = f32[1,768,256]{2,1,0:T(8,128)} fusion(bf16[8,256,768]{2,1,0:T(8,128)(2,1)} %get-tuple-element.30, bf16[256,256]{1,0:T(8,128)(2,1)S(1)} %fusion.17), kind=kOutput, calls=%fused_computation.9 | convolution fusion | flops 805306368 | bytes 4063232 | tf_op jit(solution)/shard_map/dot_general | solution.py:180
  (3 shorter events, 0.1 us)
Async XLA Ops:
  0.6 1.7 copy-start
  2.9 2.2 copy-start.3
  2.9 2.2 copy-start.4
  2.9 2.3 copy-start.1
  5.8 2.2 copy-start.2
  171.7 3.9 %copy-start.5 = (bf16[8,256,768]{2,1,0:T(8,128)(2,1)S(1)}, bf16[8,256,768]{2,1,0:T(8,128)(2,1)}, u32[]{:S(2)}) copy-start(bf16[8,256,768]{2,1,0:T(8,128)(2,1)} %get-tuple-element.26) | copy-start | bytes 9437188
  171.7 3.9 %copy-start.8 = (bf16[64,96,128]{2,1,0:T(8,128)(2,1)S(1)}, bf16[64,96,128]{2,1,0:T(8,128)(2,1)}, u32[]{:S(2)}) copy-start(bf16[64,96,128]{2,1,0:T(8,128)(2,1)} %get-tuple-element.25) | copy-start | bytes 4718596
  180.1 4.1 %copy-start.7 = (bf16[8,256,768]{2,1,0:T(8,128)(2,1)S(1)}, bf16[8,256,768]{2,1,0:T(8,128)(2,1)}, u32[]{:S(2)}) copy-start(bf16[8,256,768]{2,1,0:T(8,128)(2,1)} %get-tuple-element.27) | copy-start | bytes 9437188
  180.1 4.1 %copy-start.9 = (f32[384,768]{1,0:T(8,128)S(1)}, f32[384,768]{1,0:T(8,128)}, u32[]{:S(2)}) copy-start(f32[384,768]{1,0:T(8,128)} %convolution_bitcast_fusion.1) | copy-start | bytes 3538948
  184.2 1.9 copy-start.6

commit v10 on v7

--- a/solution.py
+++ b/solution.py
@@ -68,7 +68,30 @@
         copy = pltpu.make_async_copy(block(i, me), dsts[i].at[me], own.at[i])
         copy.start()
         local.append(copy)
+    partner = me_dp + 1 - 2 * (me_dp % 2)
+    column = sizes["dp"] // 2
+
+    def relay(i, peer, slot):
+        return pltpu.make_async_remote_copy(
+            src_ref=dsts[i].at[slot],
+            dst_ref=dsts[i].at[slot],
+            send_sem=send.at[i, sizes["dp"] + peer],
+            recv_sem=recv.at[i, slot],
+            device_id=(peer, me_ex),
+            device_id_type=pl.DeviceIdType.MESH,
+        )
+
+    gathers = [i for i, (kind, _) in enumerate(plan) if kind == "gather"]
+    for i in gathers:
+        remote(i, partner, me_dp).start()
+
+        @pl.loop(1, column)
+        def _(k):
+            remote(i, lax.rem(me_dp + 2 * k, sizes["dp"]), me_dp).start()
+
     for i, (kind, axis) in enumerate(plan):
+        if kind == "gather":
+            continue
         me, n = mine[axis], sizes[axis]
 
         @pl.loop(1, n)
@@ -76,8 +99,28 @@
             peer = lax.rem(me + turn(j, n), n)
             remote(i, peer, me).start()
 
+    for i in gathers:
+        remote(i, partner, partner).wait_recv()
+
+        @pl.loop(1, column)
+        def _(k):
+            relay(i, lax.rem(me_dp + 2 * k, sizes["dp"]), partner).start()
+
     for i, (kind, axis) in enumerate(plan):
         me, n = mine[axis], sizes[axis]
+        if kind == "gather":
+            remote(i, partner, me).wait_send()
+
+            @pl.loop(1, column)
+            def _(k):
+                peer = lax.rem(me_dp + 2 * k, sizes["dp"])
+                remote(i, peer, me).wait_send()
+                relay(i, peer, partner).wait_send()
+                remote(i, peer, peer).wait_recv()
+                twin = peer + 1 - 2 * (peer % 2)
+                remote(i, twin, twin).wait_recv()
+
+            continue
 
         @pl.loop(1, n)
         def _(j):
@@ -91,7 +134,7 @@
 
 def exchange(plan, sizes, srcs, dst_shapes, tag):
     count = len(plan)
-    most = max(sizes.values())
+    most = max(max(sizes.values()), 2 * sizes["dp"])
     return pl.pallas_call(
         functools.partial(xfer_kernel, plan, sizes),
         out_shape=[jax.ShapeDtypeStruct(s, a.dtype) for s, a in zip(dst_shapes, srcs)],

time: 296 us -> 295 us (level)
  no operation moved by 1% of the time
where the time goes in v10:
time: 295 us
  Pallas kernels  255 us (86%)
  local copies, waits for them, and re-layouts  16.6 us (6%)
  matrix products  15.2 us (5%)
  other arithmetic  7.36 us (2%)
    pallas_call x2, Pallas kernels, exchange(): pl.pallas_call(functools.partial(xfer_kernel, plan, sizes), out_shape=[ja...  255 us

profile of v10, /device:TPU:1, one launch (start us, length us, event | category | flops | bytes accessed | tf_op | source)
XLA Modules:
  0.0 294.7 jit_solution(8860326321756931233)
XLA Ops:
  0.6 0.0 copy-start
  0.6 0.9 convert_reduce_fusion.1
  1.6 0.7 multiply_add_fusion
  2.3 0.7 bitcast_add_fusion
  2.9 0.8 select_reduce_fusion.1
  3.8 1.9 copy.53
  5.7 0.0 copy-done
  5.7 0.6 multiply_convert_fusion
  6.3 0.0 copy-start.1
  6.3 2.1 copy.52
  8.5 0.0 copy-done.1
  8.5 0.6 convolution_convert_fusion.1
  9.0 2.2 copy.50
  11.2 158.2 %shard_map.94 = (bf16[64,96,128]{2,1,0:T(8,128)(2,1)}, bf16[64,96,128]{2,1,0:T(8,128)(2,1)}, bf16[8,256,768]{2,1,0:T(8,128)(2,1)}, bf16[8,256,768]{2,1,0:T(8,128)(2,1)}, bf16[8,256,768]{2,1,0:T(8,128)(2,1)}) custom-call(bf16[64,96,128]{2,1,0:T(8,128)(2,1)} %bitcast.81, bf16[64,96,128]{2,1,0:T(8,128)(2,1)} %bitcast.80, bf16[256,768]{1,0:T(8,128)(2,1)} %bitcast.91, ...), custom_call_target="tpu_custom_call" | custom-call | tf_op jit(solution)/shard_map/pallas_call | solution.py:138
  169.4 2.1 copy.59
  171.5 0.0 copy-start.3
  171.6 0.0 copy-start.6
  171.6 3.9 %convolution_bitcast_fusion = f32[384,768]{1,0:T(8,128)S(1)} fusion(bf16[16,128,768]{2,1,0:T(8,128)(2,1)} %bitcast.97, bf16[384,16,128]{2,1,0:T(8,128)(2,1)} %bitcast.100), kind=kOutput, calls=%fused_computation.5 | convolution fusion | flops 1207959552 | bytes 5898240 | tf_op jit(solution)/shard_map/dot_general | solution.py:195
  175.5 0.0 copy-done.3
  175.5 0.0 copy-done.6
  175.5 0.0 copy-start.5
  175.5 1.4 convolution_bitcast_fusion.1
  176.9 0.5 copy-done.5
  177.4 0.0 copy-start.4
  177.4 1.6 multiply_reduce_fusion
  179.0 0.2 copy-done.4
  179.3 1.6 fusion.6
  180.8 1.4 add_convert_fusion
  182.3 3.6 %convolution_convert_fusion = bf16[16,128,768]{2,1,0:T(8,128)(2,1)} fusion(bf16[384,16,128]{0,2,1:T(8,128)(2,1)S(1)} %copy.59, f32[384,768]{1,0:T(8,128)S(1)} %convolution_bitcast_fusion.1, f32[384,768]{1,0:T(8,128)S(1)} %convolution_bitcast_fusion), kind=kOutput, calls=%fused_computation.3 | convolution fusion | flops 1211301888 | bytes 7077888 | tf_op jit(solution)/shard_map/dot_general | solution.py:209
  185.8 2.2 copy.57
  188.0 0.2 convert_element_type.71
  188.1 0.7 scatter.4.refs_1_
  188.9 96.5 %shard_map.95 = (bf16[64,96,128]{2,1,0:T(8,128)(2,1)}, bf16[64,8,128]{2,1,0:T(8,128)(2,1)}, bf16[8,256,768]{2,1,0:T(8,128)(2,1)}) custom-call(bf16[64,96,128]{2,1,0:T(8,128)(2,1)} %bitcast.82, bf16[64,8,128]{2,1,0:T(8,128)(2,1)} %scatter.4.refs_1_, bf16[8,256,768]{2,1,0:T(8,128)(2,1)} %bitcast.85), custom_call_target="tpu_custom_call" | custom-call | tf_op jit(solution)/shard_map/pallas_call | solution.py:138
  285.4 2.1 copy.60
  287.5 0.6 fusion.21
  288.1 0.0 copy-start.2
  288.1 0.1 convert_element_type.66
  288.2 1.0 copy.61
  289.3 1.0 convert_reduce_fusion.2
  290.2 0.1 reshape.145
  290.4 0.1 select_reduce_fusion
  290.5 0.0 copy-done.2
  290.5 0.6 bitcast_divide_fusion
  291.1 2.4 convert_reduce_fusion
  293.5 1.1 copy.62
  (1 shorter events, 0.0 us)
Async XLA Ops:
  0.6 5.1 %copy-start = (bf16[128,2048]{1,0:T(8,128)(2,1)S(1)}, bf16[128,2048]{1,0:T(8,128)(2,1)}, u32[]{:S(2)}) copy-start(bf16[128,2048]{1,0:T(8,128)(2,1)} %param.12) | copy-start | bytes 1572868
  6.3 2.2 copy-start.1
  171.5 3.9 %copy-start.3 = (bf16[8,256,768]{2,1,0:T(8,128)(2,1)S(1)}, bf16[8,256,768]{2,1,0:T(8,128)(2,1)}, u32[]{:S(2)}) copy-start(bf16[8,256,768]{2,1,0:T(8,128)(2,1)} %get-tuple-element.26) | copy-start | bytes 9437188
  171.6 3.9 %copy-start.6 = (bf16[64,96,128]{2,1,0:T(8,128)(2,1)S(1)}, bf16[64,96,128]{2,1,0:T(8,128)(2,1)}, u32[]{:S(2)}) copy-start(bf16[64,96,128]{2,1,0:T(8,128)(2,1)} %get-tuple-element.25) | copy-start | bytes 4718596
  175.5 1.9 copy-start.5
  177.4 1.9 copy-start.4
  288.1 2.4 copy-start.2
